TPU v7x, 512 devices: a whole 4x4x16 slice. The times are simulated.
512 devices in a mesh: samp: 64 (over z, y), hour: 8 (over x, core).
Axes of the slice: x: 4, y: 4, z: 16, core: 2. Of those that a mesh axis runs over, the one named last changes fastest.
Arguments:
- load_gap: float32 [3008, 4, 256], P('samp', None, 'hour'), may hold values from -21 to 21
- profiles: bfloat16 [4, 256, 131072], P(None, 'hour', 'samp'), may hold values from 0.019897461 to 0.3984375
- slot_of_sample: int32 [131072], P('samp'), may hold values from 0 to 1023, as said below
- slot_county: int32 [64, 1024], replicated, may hold values from 0 to 3007, as said below
Outputs:
- weight_step: float32 [4, 131072], P(None, ('samp', 'hour'))
- search_dir: float32 [4, 131072], P(None, ('samp', 'hour'))
- load_dir: float32 [3008, 4, 256], P('samp', None, 'hour')
Inputs may be any that keep to these rules, and one draw needn't show every extreme that they name: `slot_of_sample`: every slot 0 to 1023 of an index of samp is used by some sample of that index. `slot_county`: row d lists 1024 distinct counties in increasing order; county c is owned by index c // 47 of samp. At most 32 counties of a row have one owner; in every draw some owner has exactly 32 counties in every row.
All inputs are finite; a program needn't handle non-finite values.
Results may differ from a plain program's by a relative error of at most 0.00062.
Values sent between devices are 32-bit elements; how exact they have to be, the bound alone decides.
A program may use at most 64 MiB of HBM per device.

v0:
```python
import functools

import jax
import jax.numpy as jnp
from jax import lax
from jax.sharding import Mesh
from jax.sharding import PartitionSpec as P

CAP = 32
SAMP = ("samp_0", "samp_1")
HOUR = ("hour_0", "hour_1")
SAMP_HOUR = ("samp_0", "samp_1", "hour_0", "hour_1")


epsilon = 1e-06


def from_everyone(x, axis):
    copies = jnp.broadcast_to(x, (lax.axis_size(axis), *x.shape))
    return lax.all_to_all(copies, axis, split_axis=0, concat_axis=0, tiled=True)


def taken_together(x, axis):
    return from_everyone(x, axis).sum(axis=0)


def one_axis_at_a_time(x, axes):
    return functools.reduce(lax.psum, axes, x)


def local(load_gap, profiles, slot_of_sample, slot_county):
    owners = lax.axis_size(SAMP)
    hour_count = lax.axis_size(HOUR)
    owner_index = lax.axis_index(SAMP)
    hour_index = lax.axis_index(HOUR)
    use_count, hour_dev, samp_dev = profiles.shape
    per_owner = load_gap.shape[0]
    slot_total = slot_county.shape[1]
    row_width = use_count * hour_dev
    share_len = samp_dev // hour_count
    space_count = float(per_owner * owners * row_width * hour_count)
    sample_count = float(use_count * samp_dev * owners)
    my_counties = lax.dynamic_index_in_dim(slot_county, owner_index, 0, keepdims=False)
    owner_of_slot = my_counties // per_owner
    lane_index = jnp.arange(CAP, dtype=jnp.int32)
    slot_index = jnp.arange(slot_total, dtype=jnp.int32)
    peer_index = jnp.arange(owners, dtype=jnp.int32)
    send_count = jnp.sum((owner_of_slot[None, :] == peer_index[:, None]).astype(jnp.int32), axis=1)
    send_start = jnp.sum((owner_of_slot[None, :] < peer_index[:, None]).astype(jnp.int32), axis=1)
    send_valid = lane_index[None, :] < send_count[:, None]
    send_index = jnp.minimum(send_start[:, None] + lane_index[None, :], slot_total - 1)
    slot_start = jnp.sum(
        (owner_of_slot[None, :] < owner_of_slot[:, None]).astype(jnp.int32), axis=1
    )
    back_index = owner_of_slot * CAP + slot_index - slot_start
    owner_table = slot_county // per_owner
    arrive_count = jnp.sum((owner_table == owner_index).astype(jnp.int32), axis=1)
    arrive_start = jnp.sum((owner_table < owner_index).astype(jnp.int32), axis=1)
    arrive_valid = lane_index[None, :] < arrive_count[:, None]
    arrive_index = jnp.minimum(arrive_start[:, None] + lane_index[None, :], slot_total - 1)
    arrive_county = jnp.take_along_axis(slot_county, arrive_index, axis=1) - owner_index * per_owner
    arrive_county = jnp.where(arrive_valid, arrive_county, -1)
    county_index = jnp.arange(per_owner, dtype=jnp.int32)
    collect = (arrive_county.reshape(-1)[None, :] == county_index[:, None]).astype(jnp.float32)
    safe_county = jnp.maximum(arrive_county, 0)

    def slot_values(owner_rows):
        outgoing = jnp.where(
            arrive_valid[:, :, None], jnp.take(owner_rows, safe_county, axis=0), 0.0
        )
        incoming = lax.all_to_all(outgoing, SAMP, split_axis=0, concat_axis=0, tiled=True)
        return jnp.take(incoming.reshape(owners * CAP, row_width), back_index, axis=0)

    def backward_terms(slot_rows):
        spread = jnp.take(slot_rows.T, slot_of_sample, axis=1).reshape(
            use_count, hour_dev, samp_dev
        )
        return jnp.sum(profiles.astype(jnp.float32) * spread, axis=1)

    def hour_total(partial_value):
        summed = taken_together(partial_value, HOUR)
        return (lax.dynamic_slice_in_dim(summed, hour_index * share_len, share_len, 1), summed)

    def global_sums(values):
        return jax.tree.map(lambda part: one_axis_at_a_time(part, SAMP_HOUR), values)

    gap_rows = load_gap.reshape(per_owner, row_width)
    gap_square = jnp.sum(gap_rows * gap_rows)
    plain_share, plain_whole = hour_total(backward_terms(slot_values(gap_rows)))
    gap_total, plain_total = global_sums((gap_square, jnp.sum(plain_share * plain_share)))
    beta_one = jnp.sqrt(gap_total / space_count + epsilon)
    first_load = gap_rows / beta_one
    image_share = plain_share / beta_one
    image_whole = plain_whole / beta_one
    alpha_one = jnp.sqrt(plain_total / (beta_one * beta_one) / sample_count + epsilon)
    vector_share = image_share / alpha_one
    vector_whole = image_whole / alpha_one
    weighted = (profiles.astype(jnp.float32) * vector_whole[:, None, :]).astype(jnp.bfloat16)
    weighted = weighted.reshape(row_width, samp_dev)
    block_size = min(samp_dev, 2048)
    picked = (slot_of_sample[0:block_size, None] == slot_index[None, :]).astype(jnp.bfloat16)
    running = lax.dot_general(
        picked, weighted, (((0,), (1,)), ((), ())), preferred_element_type=jnp.float32
    )
    outgoing = jnp.where(send_valid[:, :, None], jnp.take(running, send_index, axis=0), 0.0)
    incoming = lax.all_to_all(outgoing, SAMP, split_axis=0, concat_axis=0, tiled=True)
    mismatch = (
        jnp.dot(
            collect,
            incoming.reshape(owners * CAP, row_width),
            precision=lax.Precision.HIGHEST,
            preferred_element_type=jnp.float32,
        )
        - alpha_one * first_load
    )
    (mismatch_total,) = global_sums((jnp.sum(mismatch * mismatch),))
    beta_two = jnp.sqrt(mismatch_total / space_count + epsilon)
    load_dir = mismatch / beta_two
    back_share, back_whole = hour_total(backward_terms(slot_values(load_dir)))
    image_two = back_share - beta_two * vector_share
    (second_total,) = global_sums((jnp.sum(image_two * image_two),))
    alpha_two = jnp.sqrt(second_total / sample_count + epsilon)
    vector_two = image_two / alpha_two
    rho_value = jnp.sqrt(alpha_one * alpha_one + beta_two * beta_two)
    cosine = alpha_one / rho_value
    sine = beta_two / rho_value
    weight_step = cosine * beta_one / rho_value * vector_share
    search_dir = vector_two - sine * alpha_two / rho_value * vector_share
    return (weight_step, search_dir, load_dir.reshape(per_owner, use_count, hour_dev))


def solution(mesh):
    finer = Mesh(mesh.devices.reshape(16, 4, 4, 2), ("samp_0", "samp_1", "hour_0", "hour_1"))
    return jax.shard_map(
        local,
        mesh=finer,
        in_specs=(P(SAMP, None, HOUR), P(None, HOUR, SAMP), P(SAMP), P()),
        out_specs=(P(None, SAMP_HOUR), P(None, SAMP_HOUR), P(SAMP, None, HOUR)),
        check_vma=False,
    )
```

profile of v0, /device:TPU:1, one launch (start us, length us, event | category | flops | bytes accessed | tf_op | source)
XLA Modules:
  0.0 444.5 jit_solution(9064519694770817467)
XLA Ops:
  2.2 16.6 %gather_fusion.1 = s32[2048]{0:T(1024)S(1)} fusion(s32[64,1024]{1,0:T(8,128)S(1)} %copy-done, s32[2048]{0:T(1024)S(1)} %reshape.340), kind=kCustom, calls=%fused_computation.7 | custom fusion | bytes 32768 | tf_op jit(solution)/shard_map/jit(take_along_axis)/gather | solution.py:61
  19.1 5.5 %gather_fusion.2 = f32[2048,128]{1,0:T(8,128)S(1)} fusion(f32[47,128]{1,0:T(8,128)S(1)} %copy.25, s32[2048]{0:T(1024)S(1)} %broadcast_clamp_fusion.1), kind=kCustom, calls=%fused_computation.clone | custom fusion | bytes 2105344 | tf_op jit(solution)/shard_map/jit(_take)/gather | solution.py:69
  26.2 19.4 %all-to-all-start = ((f32[64,32,128]{2,1,0:T(8,128)}), f32[64,32,128]{2,1,0:T(8,128)S(1)}, u32[]{:S(2)}, u32[]{:S(2)}) async-start(f32[64,32,128]{2,1,0:T(8,128)} %select_select_fusion.1), calls=%async_computation | async-start | bytes 2097152 | tf_op jit(solution)/shard_map/all_to_all | solution.py:71
  46.5 50.5 %all-to-all-done = f32[64,32,128]{2,1,0:T(8,128)S(1)} async-done(((f32[64,32,128]{2,1,0:T(8,128)}), f32[64,32,128]{2,1,0:T(8,128)S(1)}, u32[]{:S(2)}, u32[]{:S(2)}) %all-to-all-start) | async-done | bytes 1048608 | tf_op jit(solution)/shard_map/all_to_all | solution.py:71
  100.1 5.5 %gather_fusion.4 = f32[2048,128]{1,0:T(8,128)S(1)} fusion(f32[128,1024]{0,1:T(8,128)S(1)} %select_bitcast_fusion.3, s32[2048]{0:T(1024)S(1)} %fusion.18), kind=kCustom, calls=%fused_computation.2.clone | custom fusion | bytes 2105344 | tf_op jit(solution)/shard_map/jit(_take)/gather | solution.py:75
  107.8 9.1 %all-to-all-start.1 = ((f32[8,4,2048]{2,1,0:T(4,128)}), f32[8,4,2048]{2,1,0:T(4,128)S(1)}, u32[]{:S(2)}, u32[]{:S(2)}) async-start(f32[8,4,2048]{2,1,0:T(4,128)} %broadcast_in_dim.102), calls=%async_computation.1 | async-start | bytes 524288 | tf_op jit(solution)/shard_map/all_to_all | solution.py:20
  117.7 5.7 %all-to-all-done.1 = f32[8,4,2048]{2,1,0:T(4,128)S(1)} async-done(((f32[8,4,2048]{2,1,0:T(4,128)}), f32[8,4,2048]{2,1,0:T(4,128)S(1)}, u32[]{:S(2)}, u32[]{:S(2)}) %all-to-all-start.1) | async-done | bytes 262176 | tf_op jit(solution)/shard_map/all_to_all | solution.py:20
  124.1 20.8 %all-reduce = (f32[]{:T(128)}, f32[]{:T(128)}) all-reduce(f32[]{:T(128)} %multiply_reduce_fusion.3, f32[]{:T(128)} %multiply_reduce_fusion), channel_id=1, replica_groups=mesh['samp_0'=16,'samp_1'=4,'hour_0'=4,'hour_1'=2] {'samp_0'}, use_global_device_ids=true, to_apply=%region_6.10 | all-reduce | flops 2 | bytes 16 | tf_op jit(solution)/shard_map/psum | solution.py:28
  144.9 9.2 %all-reduce.2 = (f32[]{:T(128)}, f32[]{:T(128)}) all-reduce(f32[]{:T(128)} %get-tuple-element.22, f32[]{:T(128)} %get-tuple-element.23), channel_id=1, replica_groups=mesh['samp_0'=16,'samp_1'=4,'hour_0'=4,'hour_1'=2] {'samp_1'}, use_global_device_ids=true, to_apply=%region_7.11 | all-reduce | flops 2 | bytes 16 | tf_op jit(solution)/shard_map/psum | solution.py:28
  154.1 7.5 %all-reduce.1 = (f32[]{:T(128)}, f32[]{:T(128)}) all-reduce(f32[]{:T(128)} %get-tuple-element.26, f32[]{:T(128)} %get-tuple-element.27), channel_id=1, replica_groups=mesh['samp_0'=16,'samp_1'=4,'hour_0'=4,'hour_1'=2] {'hour_0'}, use_global_device_ids=true, to_apply=%region_8.12 | all-reduce | flops 2 | bytes 16 | tf_op jit(solution)/shard_map/psum | solution.py:28
  161.6 14.5 %all-reduce.3 = (f32[]{:T(128)}, f32[]{:T(128)}) all-reduce(f32[]{:T(128)} %get-tuple-element.24, f32[]{:T(128)} %get-tuple-element.25), channel_id=1, replica_groups=mesh['samp_0'=16,'samp_1'=4,'hour_0'=4,'hour_1'=2] {'hour_1'}, use_global_device_ids=true, to_apply=%region_9.13 | all-reduce | flops 2 | bytes 16 | tf_op jit(solution)/shard_map/psum | solution.py:28
  186.3 6.2 %all-to-all-start.2 = ((f32[64,32,128]{2,1,0:T(8,128)}), f32[64,32,128]{2,1,0:T(8,128)S(1)}, u32[]{:S(2)}, u32[]{:S(2)}) async-start(f32[64,32,128]{2,1,0:T(8,128)} %select_select_fusion.2), calls=%async_computation.2 | async-start | bytes 2097152 | tf_op jit(solution)/shard_map/all_to_all | solution.py:106
  192.8 52.2 %all-to-all-done.2 = f32[64,32,128]{2,1,0:T(8,128)S(1)} async-done(((f32[64,32,128]{2,1,0:T(8,128)}), f32[64,32,128]{2,1,0:T(8,128)S(1)}, u32[]{:S(2)}, u32[]{:S(2)}) %all-to-all-start.2) | async-done | bytes 1048608 | tf_op jit(solution)/shard_map/all_to_all | solution.py:106
  246.2 22.3 %psum.120 = f32[]{:T(128)} all-reduce(f32[]{:T(128)} %get-tuple-element.39), channel_id=1, replica_groups=mesh['samp_0'=16,'samp_1'=4,'hour_0'=4,'hour_1'=2] {'samp_0'}, use_global_device_ids=true, to_apply=%region_18.22 | all-reduce | flops 1 | bytes 8 | tf_op jit(solution)/shard_map/psum | solution.py:28
  268.5 9.2 %psum.121 = f32[]{:T(128)} all-reduce(f32[]{:T(128)} %psum.120), channel_id=1, replica_groups=mesh['samp_0'=16,'samp_1'=4,'hour_0'=4,'hour_1'=2] {'samp_1'}, use_global_device_ids=true, to_apply=%region_19.23 | all-reduce | flops 1 | bytes 8 | tf_op jit(solution)/shard_map/psum | solution.py:28
  277.7 7.2 %psum.122 = f32[]{:T(128)} all-reduce(f32[]{:T(128)} %psum.121), channel_id=1, replica_groups=mesh['samp_0'=16,'samp_1'=4,'hour_0'=4,'hour_1'=2] {'hour_0'}, use_global_device_ids=true, to_apply=%region_20.24 | all-reduce | flops 1 | bytes 8 | tf_op jit(solution)/shard_map/psum | solution.py:28
  284.9 15.7 %psum.123 = f32[]{:T(128)} all-reduce(f32[]{:T(128)} %psum.122), channel_id=1, replica_groups=mesh['samp_0'=16,'samp_1'=4,'hour_0'=4,'hour_1'=2] {'hour_1'}, use_global_device_ids=true, to_apply=%region_21.25 | all-reduce | flops 1 | bytes 8 | tf_op jit(solution)/shard_map/psum | solution.py:28
  307.5 58.4 %all_to_all.25 = f32[64,32,128]{2,1,0:T(8,128)S(1)} all-to-all(f32[64,32,128]{2,1,0:T(8,128)S(1)} %select_select_fusion), channel_id=1, replica_groups=mesh['samp_0'=16,'samp_1'=4,'hour_0'=4,'hour_1'=2] {'samp_0','samp_1'}, dimensions={0} | all-to-all | bytes 2097152 | tf_op jit(solution)/shard_map/all_to_all | solution.py:71
  376.0 7.0 %all-to-all-start.4 = ((f32[8,4,2048]{2,1,0:T(4,128)}), f32[8,4,2048]{2,1,0:T(4,128)S(1)}, u32[]{:S(2)}, u32[]{:S(2)}) async-start(f32[8,4,2048]{2,1,0:T(4,128)} %broadcast_in_dim.108), calls=%async_computation.4 | async-start | bytes 524288 | tf_op jit(solution)/shard_map/all_to_all | solution.py:20
  383.1 6.4 %all-to-all-done.4 = f32[8,4,2048]{2,1,0:T(4,128)S(1)} async-done(((f32[8,4,2048]{2,1,0:T(4,128)}), f32[8,4,2048]{2,1,0:T(4,128)S(1)}, u32[]{:S(2)}, u32[]{:S(2)}) %all-to-all-start.4) | async-done | bytes 262176 | tf_op jit(solution)/shard_map/all_to_all | solution.py:20
  390.3 20.8 %psum.124 = f32[]{:T(128)} all-reduce(f32[]{:T(128)} %multiply_reduce_fusion.2), channel_id=1, replica_groups=mesh['samp_0'=16,'samp_1'=4,'hour_0'=4,'hour_1'=2] {'samp_0'}, use_global_device_ids=true, to_apply=%region_25.29 | all-reduce | flops 1 | bytes 8 | tf_op jit(solution)/shard_map/psum | solution.py:28
  411.8 8.9 %psum.125 = f32[]{:T(128)} all-reduce(f32[]{:T(128)} %psum.124), channel_id=1, replica_groups=mesh['samp_0'=16,'samp_1'=4,'hour_0'=4,'hour_1'=2] {'samp_1'}, use_global_device_ids=true, to_apply=%region_26.30 | all-reduce | flops 1 | bytes 8 | tf_op jit(solution)/shard_map/psum | solution.py:28
  420.7 7.5 %psum.126 = f32[]{:T(128)} all-reduce(f32[]{:T(128)} %psum.125), channel_id=1, replica_groups=mesh['samp_0'=16,'samp_1'=4,'hour_0'=4,'hour_1'=2] {'hour_0'}, use_global_device_ids=true, to_apply=%region_27.31 | all-reduce | flops 1 | bytes 8 | tf_op jit(solution)/shard_map/psum | solution.py:28
  428.2 15.0 %psum.127 = f32[]{:T(128)} all-reduce(f32[]{:T(128)} %psum.126), channel_id=1, replica_groups=mesh['samp_0'=16,'samp_1'=4,'hour_0'=4,'hour_1'=2] {'hour_1'}, use_global_device_ids=true, to_apply=%region_28.32 | all-reduce | flops 1 | bytes 8 | tf_op jit(solution)/shard_map/psum | solution.py:28
  (65 shorter events, 39.5 us)
Async XLA Ops:
  0.6 1.5 copy-start
  2.2 16.9 %copy-start.2 = (f32[47,4,32]{0,2,1:T(8,128)S(1)}, f32[47,4,32]{0,2,1:T(8,128)}, u32[]{:S(2)}) copy-start(f32[47,4,32]{0,2,1:T(8,128)} %param.10) | copy-start | bytes 72196
  26.2 20.3 %copy-start.3 = (s32[2048]{0:T(1024)S(1)}, s32[2048]{0:T(1024)}, u32[]{:S(2)}) copy-start(s32[2048]{0:T(1024)} %param.12) | copy-start | bytes 24580
  26.2 70.9 %all-to-all-start = ((f32[64,32,128]{2,1,0:T(8,128)}), f32[64,32,128]{2,1,0:T(8,128)S(1)}, u32[]{:S(2)}, u32[]{:S(2)}) async-start(f32[64,32,128]{2,1,0:T(8,128)} %select_select_fusion.1), calls=%async_computation | async-start | bytes 2097152 | tf_op jit(solution)/shard_map/all_to_all | solution.py:71
  105.9 1.0 copy-start.1
  107.8 15.6 %all-to-all-start.1 = ((f32[8,4,2048]{2,1,0:T(4,128)}), f32[8,4,2048]{2,1,0:T(4,128)S(1)}, u32[]{:S(2)}, u32[]{:S(2)}) async-start(f32[8,4,2048]{2,1,0:T(4,128)} %broadcast_in_dim.102), calls=%async_computation.1 | async-start | bytes 524288 | tf_op jit(solution)/shard_map/all_to_all | solution.py:20
  186.3 58.8 %all-to-all-start.2 = ((f32[64,32,128]{2,1,0:T(8,128)}), f32[64,32,128]{2,1,0:T(8,128)S(1)}, u32[]{:S(2)}, u32[]{:S(2)}) async-start(f32[64,32,128]{2,1,0:T(8,128)} %select_select_fusion.2), calls=%async_computation.2 | async-start | bytes 2097152 | tf_op jit(solution)/shard_map/all_to_all | solution.py:106
  376.0 13.5 %all-to-all-start.4 = ((f32[8,4,2048]{2,1,0:T(4,128)}), f32[8,4,2048]{2,1,0:T(4,128)S(1)}, u32[]{:S(2)}, u32[]{:S(2)}) async-start(f32[8,4,2048]{2,1,0:T(4,128)} %broadcast_in_dim.108), calls=%async_computation.4 | async-start | bytes 524288 | tf_op jit(solution)/shard_map/all_to_all | solution.py:20
where the time goes:
time: 445 us
  blocking collectives  217 us (49%)
  waiting for transfers between devices  115 us (26%)
  local copies, waits for them, and re-layouts  53.9 us (12%)
  starting transfers between devices  41.7 us (9%)
  other arithmetic  10.4 us (2%)
    psum x12, blocking collectives, one_axis_at_a_time(): return functools.reduce(lax.psum, axes, x)  159 us
    all_to_all x1, blocking collectives, slot_values(): lax.all_to_all(outgoing, SAMP, split_axis=0, concat_axis=0, tiled=True)  58.4 us
    all_to_all x1, waiting for transfers between devices, local(): lax.all_to_all(outgoing, SAMP, split_axis=0, concat_axis=0, tiled=True)  52.2 us
    all_to_all x1, waiting for transfers between devices, slot_values(): lax.all_to_all(outgoing, SAMP, split_axis=0, concat_axis=0, tiled=True)  50.5 us
    all_to_all x1, starting transfers between devices, slot_values(): lax.all_to_all(outgoing, SAMP, split_axis=0, concat_axis=0, tiled=True)  19.4 us
    gather x3, local copies, waits for them, and re-layouts, local(): jnp.take_along_axis(slot_county, arrive_index, axis=1)  16.8 us
    all_to_all x2, starting transfers between devices, from_everyone(): return lax.all_to_all(copies, axis, split_axis=0, concat_axis=0, tiled=True)  16.1 us
    all_to_all x2, waiting for transfers between devices, from_everyone(): return lax.all_to_all(copies, axis, split_axis=0, concat_axis=0, tiled=True)  12.2 us
  transfers between devices with their start and end apart: 4, of which 4 were waited for; matrix products, arithmetic and copies ran while one was open for 0% of the time, Pallas kernels for 0%

commit v1 on v0

v1 whole, which is shorter than its diff:
```python
import jax
import jax.numpy as jnp
from jax import lax
from jax.sharding import PartitionSpec as P

epsilon = 1e-06
PAD = 48


def two_pieces(x, axis):
    high = lax.reduce_precision(x, 8, 7)
    return jnp.concatenate([high, x - high], axis=axis).astype(jnp.bfloat16)


def local(load_gap, profiles, slot_of_sample, slot_county):
    owners = lax.axis_size("samp")
    hour_count = lax.axis_size("hour")
    owner_index = lax.axis_index("samp")
    hour_index = lax.axis_index("hour")
    use_count, hour_dev, samp_dev = profiles.shape
    per_owner = load_gap.shape[0]
    row_width = use_count * hour_dev
    share_len = samp_dev // hour_count
    space_count = float(per_owner * owners * row_width * hour_count)
    sample_count = float(use_count * samp_dev * owners)
    my_counties = lax.dynamic_index_in_dim(slot_county, owner_index, 0, keepdims=False)
    county = jnp.take(my_counties, slot_of_sample)
    place = county // per_owner * PAD + county % per_owner
    places = jnp.arange(owners * PAD, dtype=jnp.int32)
    onehot = (places[:, None] == place[None, :]).astype(jnp.bfloat16)
    wide = profiles.astype(jnp.float32)

    def padded(rows):
        return jnp.pad(rows, ((0, PAD - per_owner), (0, 0)))

    def backward(rows):
        everyone = lax.all_gather(padded(rows), "samp", tiled=True)
        square = jnp.sum(everyone * everyone)
        pieces = two_pieces(everyone, 1)
        spread = lax.dot_general(
            pieces, onehot, (((0,), (0,)), ((), ())), preferred_element_type=jnp.float32
        )
        spread = (spread[:row_width] + spread[row_width:]).reshape(use_count, hour_dev, samp_dev)
        partial = jnp.sum(wide * spread, axis=1)
        extra = jnp.zeros((1, samp_dev), jnp.float32).at[0, 0].set(square)
        total = lax.psum(jnp.concatenate([partial, extra], axis=0), "hour")
        return total[:use_count], total[use_count, 0]

    def my_share(x):
        return lax.dynamic_slice_in_dim(x, hour_index * share_len, share_len, 1)

    gap_rows = load_gap.reshape(per_owner, row_width)
    plain, gap_total = backward(gap_rows)
    beta_one = jnp.sqrt(gap_total / space_count + epsilon)
    image = plain / beta_one
    weighted = (wide * image[:, None, :]).reshape(row_width, samp_dev)
    sums = lax.dot_general(
        onehot, two_pieces(weighted, 0), (((1,), (1,)), ((), ())), preferred_element_type=jnp.float32
    )
    sums = (sums[:, :row_width] + sums[:, row_width:]).reshape(owners, PAD, row_width)
    mine = jnp.sum(image * image)
    row = jnp.arange(PAD, dtype=jnp.int32)[None, :, None]
    sums = jnp.where(row == per_owner, mine, sums).reshape(owners * PAD, row_width)
    owned = lax.psum_scatter(sums, "samp", scatter_dimension=0, tiled=True)
    alpha_one = jnp.sqrt(owned[per_owner, 0] / sample_count + epsilon)
    mismatch = owned[:per_owner] / alpha_one - (alpha_one / beta_one) * gap_rows
    back, mismatch_total = backward(mismatch)
    beta_two = jnp.sqrt(mismatch_total / space_count + epsilon)
    load_dir = mismatch / beta_two
    vector_one = image / alpha_one
    image_two = back / beta_two - beta_two * vector_one
    second_total = lax.psum(jnp.sum(image_two * image_two), "samp")
    alpha_two = jnp.sqrt(second_total / sample_count + epsilon)
    rho_value = jnp.sqrt(alpha_one * alpha_one + beta_two * beta_two)
    cosine = alpha_one / rho_value
    sine = beta_two / rho_value
    vector_share = my_share(vector_one)
    weight_step = cosine * beta_one / rho_value * vector_share
    search_dir = my_share(image_two) / alpha_two - sine * alpha_two / rho_value * vector_share
    return (weight_step, search_dir, load_dir.reshape(per_owner, use_count, hour_dev))


def solution(mesh):
    return jax.shard_map(
        local,
        mesh=mesh,
        in_specs=(P("samp", None, "hour"), P(None, "hour", "samp"), P("samp"), P()),
        out_specs=(P(None, ("samp", "hour")), P(None, ("samp", "hour")), P("samp", None, "hour")),
        check_vma=False,
    )
```

time: 445 us -> 1210 us (2.72)
  the two profiles are of different devices: /device:TPU:1 before, /device:TPU:8 now
where the time goes in v1:
time: 1210 us
  waiting for transfers between devices  962 us (80%)
  blocking collectives  188 us (16%)
  between operations  19.5 us (2%)
  matrix products  14.8 us (1%)
  local copies, waits for them, and re-layouts  13.8 us (1%)
  other arithmetic  12.8 us (1%)
    reduce_scatter x1, waiting for transfers between devices, local(): owned = lax.psum_scatter(sums, 'samp', scatter_dimension=0, tiled=True)  688 us
    all_gather x2, waiting for transfers between devices, backward(): everyone = lax.all_gather(padded(rows), 'samp', tiled=True)  274 us
    psum x1, blocking collectives, local(): second_total = lax.psum(jnp.sum(image_two * image_two), 'samp')  140 us
    psum x2, blocking collectives, backward(): total = lax.psum(jnp.concatenate([partial, extra], axis=0), 'hour')  48.1 us
  transfers between devices with their start and end apart: 3, of which 3 were waited for; matrix products, arithmetic and copies ran while one was open for 1% of the time, Pallas kernels for 0%

profile of v1, /device:TPU:8, one launch (start us, length us, event | category | flops | bytes accessed | tf_op | source)
XLA Modules:
  0.0 1211.6 jit_solution(9387377253845586838)
XLA Ops:
  7.2 0.9 copy.11
  8.2 0.6 pad.18
  9.0 0.7 fusion.25
  9.7 8.6 gather_fusion
  18.3 0.6 compare_reduce_fusion
  19.0 136.3 %all-gather.3.cloned.1.call-done = f32[3072,128]{1,0:T(8,128)} async-done(((f32[48,128]{1,0:T(8,128)}), f32[3072,128]{1,0:T(8,128)}) %all-gather.3.cloned.1.call-update) | async-done | bytes 1572880 | tf_op jit(solution)/shard_map/all_gather | solution.py:37
  155.2 2.4 reduce-precision_convert_fusion.1
  159.0 4.9 fusion.2
  164.2 24.1 %psum.21 = f32[5,2048]{1,0:T(8,128)S(1)} all-reduce(f32[5,2048]{1,0:T(8,128)S(1)} %select_maximum_fusion.1), channel_id=1, replica_groups=mesh['samp'=64,'hour'=8] {'hour'}, use_global_device_ids=true, to_apply=%region_3.4 | all-reduce | flops 10240 | bytes 81920 | tf_op jit(solution)/shard_map/psum | solution.py:46
  189.6 0.6 multiply_reduce_fusion.3
  190.5 4.9 fusion.1
  195.4 3.1 fusion.8
  198.6 687.6 %reduce-scatter.2.cloned.1.call-done = f32[48,128]{1,0:T(8,128)} async-done(((f32[3072,128]{1,0:T(8,128)}), f32[48,128]{1,0:T(8,128)}) %reduce-scatter.2.cloned.1.call-update) | async-done | bytes 24592 | tf_op jit(solution)/shard_map/reduce_scatter | solution.py:64
  886.2 1.2 slice.88
  888.1 0.7 fusion.21
  888.9 0.6 pad.19
  889.5 138.2 %all-gather.5.cloned.1.call-done = f32[3072,128]{1,0:T(8,128)} async-done(((f32[48,128]{1,0:T(8,128)}), f32[3072,128]{1,0:T(8,128)}) %all-gather.5.cloned.1.call-update) | async-done | bytes 1572880 | tf_op jit(solution)/shard_map/all_gather | solution.py:37
  1027.7 2.4 reduce-precision_convert_fusion
  1031.4 4.9 fusion
  1036.7 23.9 %psum.22 = f32[5,2048]{1,0:T(8,128)S(1)} all-reduce(f32[5,2048]{1,0:T(8,128)S(1)} %select_maximum_fusion), channel_id=1, replica_groups=mesh['samp'=64,'hour'=8] {'hour'}, use_global_device_ids=true, to_apply=%region_8.9 | all-reduce | flops 10240 | bytes 81920 | tf_op jit(solution)/shard_map/psum | solution.py:46
  1062.0 0.6 multiply_reduce_fusion.2
  1062.6 140.4 %psum.23 = f32[]{:T(128)} all-reduce(f32[]{:T(128)} %get-tuple-element.33), channel_id=1, replica_groups=mesh['samp'=64,'hour'=8] {'samp'}, use_global_device_ids=true, to_apply=%region_10.11 | all-reduce | flops 1 | bytes 8 | tf_op jit(solution)/shard_map/psum | solution.py:72
  1203.7 0.7 copy.12
  1204.5 0.6 divide_subtract_fusion.1
  (26 shorter events, 2.2 us)
Async XLA Ops:
  7.2 1.8 copy-start
  7.2 148.1 %all-gather.3.cloned.1.call-start = ((), (), s32[]{:S(2)}) async-start(), calls=%async_computation.1 | async-start | bytes 1597440 | tf_op jit(solution)/shard_map/all_gather | solution.py:37
  8.8 877.4 %reduce-scatter.2.cloned.1.call-start = ((), (), s32[]{:S(2)}) async-start(), calls=%async_computation.2 | async-start | bytes 1597440 | tf_op jit(solution)/shard_map/reduce_scatter | solution.py:64
  9.7 9.2 copy-start.2
  159.0 5.0 copy-start.1
  198.5 829.1 %all-gather.5.cloned.1.call-start = ((), (), s32[]{:S(2)}) async-start(), calls=%async_computation.3 | async-start | bytes 1597440 | tf_op jit(solution)/shard_map/all_gather | solution.py:37
Sparse Core Ops, SparseCore 0:
  11.5 143.6 all-gather.2
  198.7 687.4 reduce-scatter.1
  890.1 137.4 all-gather.4

commit v2 on v1

--- a/solution.py
+++ b/solution.py
@@ -1,10 +1,292 @@
 import jax
 import jax.numpy as jnp
 from jax import lax
+from jax.experimental import pallas as pl
+from jax.experimental.pallas import tpu as pltpu
 from jax.sharding import PartitionSpec as P
 
 epsilon = 1e-06
 PAD = 48
+MESH = pl.DeviceIdType.MESH
+NY = 4
+NZ = 16
+UP = NZ // 2
+DOWN = NZ - 1 - UP
+
+
+def remote(src, dst, send_sem, recv_sem, **device):
+    return pltpu.make_async_remote_copy(
+        src_ref=src, dst_ref=dst, send_sem=send_sem, recv_sem=recv_sem,
+        device_id=device, device_id_type=MESH,
+    )
+
+
+def at_place(z, y):
+    return lax.rem(z + NZ, NZ) * NY + lax.rem(y + NY, NY)
+
+
+def greet(axis, peers):
+    barrier = pltpu.get_barrier_semaphore()
+    for peer in peers:
+        pl.semaphore_signal(barrier, inc=1, device_id={axis: peer}, device_id_type=MESH)
+    return len(peers)
+
+
+def near_peers(z, y):
+    return [at_place(z, y + d) for d in range(1, NY)] + [at_place(z + 1, y), at_place(z - 1, y)]
+
+
+def gather_body(in_ref, out_ref, send_y, recv_y, send_z, recv_z):
+    me = lax.axis_index("samp")
+    z, y = me // NY, lax.rem(me, NY)
+
+    def y_copy(d):
+        return remote(in_ref, out_ref.at[me], send_y.at[d], recv_y.at[d], samp=at_place(z, y + d))
+
+    def y_arrival(d):
+        slot = out_ref.at[at_place(z, y - d)]
+        return remote(slot, slot, send_y.at[d], recv_y.at[d], samp=at_place(z, y + d))
+
+    def z_copy(way, k, j, own=False):
+        step = 1 - 2 * way
+        slot = out_ref.at[at_place(z - step * k, y - j)]
+        return remote(
+            in_ref if own else slot, slot, send_z.at[way, k, j], recv_z.at[way, k, j],
+            samp=at_place(z + step, y),
+        )
+
+    def z_arrival(way, k, j):
+        step = 1 - 2 * way
+        slot = out_ref.at[at_place(z - step * (k + 1), y - j)]
+        return remote(slot, slot, send_z.at[way, k, j], recv_z.at[way, k, j], samp=at_place(z + step, y))
+
+    z_copy(0, 0, 0, True).start()
+    z_copy(1, 0, 0, True).start()
+    for d in (2, 1, 3):
+        y_copy(d).start()
+    out_ref[pl.ds(me, 1)] = in_ref[...][None]
+    for j in (1, 3, 2):
+        y_arrival(j).wait_recv()
+        z_copy(0, 0, j).start()
+        z_copy(1, 0, j).start()
+
+    def hop(k, carry):
+        for j in (0, 1, 3, 2):
+            for way in (0, 1):
+                z_arrival(way, k - 1, j).wait_recv()
+                z_copy(way, k, j).start()
+        return carry
+
+    lax.fori_loop(1, DOWN, hop, 0)
+    for j in (0, 1, 3, 2):
+        z_arrival(0, UP - 2, j).wait_recv()
+        z_copy(0, UP - 1, j).start()
+        z_arrival(1, DOWN - 1, j).wait_recv()
+    for d in (2, 1, 3):
+        y_copy(d).wait_send()
+    z_copy(0, 0, 0, True).wait_send()
+    z_copy(1, 0, 0, True).wait_send()
+    for j in (1, 3, 2):
+        z_copy(0, 0, j).wait_send()
+        z_copy(1, 0, j).wait_send()
+
+    def drain(k, carry):
+        for j in (0, 1, 3, 2):
+            for way in (0, 1):
+                z_copy(way, k, j).wait_send()
+        return carry
+
+    lax.fori_loop(1, DOWN, drain, 0)
+    for j in (0, 1, 3, 2):
+        z_copy(0, UP - 1, j).wait_send()
+        z_arrival(0, UP - 1, j).wait_recv()
+
+
+def gather_kernel(in_ref, out_ref, got, send_y, recv_y, send_z, recv_z):
+    me = lax.axis_index("samp")
+    z, y = me // NY, lax.rem(me, NY)
+    pl.semaphore_wait(pltpu.get_barrier_semaphore(), greet("samp", near_peers(z, y)))
+    gather_body(in_ref, got, send_y, recv_y, send_z, recv_z)
+    out_ref[...] = got[...]
+
+
+def vmem(count):
+    return [pl.BlockSpec(memory_space=pltpu.VMEM)] * count
+
+
+def everyone_of(rows, number):
+    count = NY * NZ
+    dma = pltpu.SemaphoreType.DMA
+    return pl.pallas_call(
+        gather_kernel,
+        out_shape=jax.ShapeDtypeStruct((count, *rows.shape), jnp.float32),
+        in_specs=vmem(1),
+        out_specs=vmem(1)[0],
+        scratch_shapes=[
+            pltpu.VMEM((count, *rows.shape), jnp.float32),
+            dma((NY,)), dma((NY,)), dma((2, UP, NY)), dma((2, UP, NY)),
+        ],
+        compiler_params=pltpu.CompilerParams(collective_id=number, has_side_effects=True),
+    )(rows).reshape(count * rows.shape[0], rows.shape[1])
+
+
+def scatter_kernel(in_ref, out_ref, held, total, arrived, send_y, recv_y, send_z, recv_z):
+    me = lax.axis_index("samp")
+    z, y = me // NY, lax.rem(me, NY)
+    order = (2, 1, 3, 0)
+
+    def z_copy(way, k, j, own=False):
+        step = 1 - 2 * way
+        far = (UP, DOWN)[way] - k
+        src = in_ref.at[at_place(z + step * far, y + j)] if own else held.at[way, k - 1, j]
+        return remote(
+            src, held.at[way, k, j], send_z.at[way, k, j], recv_z.at[way, k, j],
+            samp=at_place(z + step, y),
+        )
+
+    def z_arrival(way, k, j):
+        step = 1 - 2 * way
+        slot = held.at[way, k, j]
+        return remote(slot, slot, send_z.at[way, k, j], recv_z.at[way, k, j], samp=at_place(z + step, y))
+
+    def add_own(way, k, j):
+        step = 1 - 2 * way
+        far = (UP, DOWN)[way] - k
+        z_arrival(way, k - 1, j).wait_recv()
+        held[way, k - 1, j] = held[way, k - 1, j] + in_ref[at_place(z + step * far, y + j)]
+        z_copy(way, k, j).start()
+
+    def y_copy(d):
+        return remote(total.at[d], arrived.at[d], send_y.at[d], recv_y.at[d], samp=at_place(z, y + d))
+
+    pl.semaphore_wait(pltpu.get_barrier_semaphore(), greet("samp", near_peers(z, y)))
+    for j in order:
+        for way in (0, 1):
+            z_copy(way, 0, j, True).start()
+
+    def hop(k, carry):
+        for j in order:
+            for way in (0, 1):
+                add_own(way, k, j)
+        return carry
+
+    lax.fori_loop(1, DOWN, hop, 0)
+    for j in order:
+        add_own(0, UP - 1, j)
+    for j in order:
+        z_arrival(1, DOWN - 1, j).wait_recv()
+        z_arrival(0, UP - 1, j).wait_recv()
+        total[j] = held[0, UP - 1, j] + held[1, DOWN - 1, j] + in_ref[at_place(z, y + j)]
+        if j:
+            y_copy(j).start()
+
+    def drain(k, carry):
+        for j in order:
+            for way in (0, 1):
+                z_copy(way, k, j).wait_send()
+        return carry
+
+    for j in order:
+        for way in (0, 1):
+            z_copy(way, 0, j, True).wait_send()
+    lax.fori_loop(1, DOWN, drain, 0)
+    for j in order:
+        z_copy(0, UP - 1, j).wait_send()
+    for d in (1, 3, 2):
+        y_copy(d).wait()
+    out_ref[...] = total[0] + arrived[1] + arrived[2] + arrived[3]
+
+
+def owned_of(sums, number):
+    block = sums.shape[1:]
+    dma = pltpu.SemaphoreType.DMA
+    return pl.pallas_call(
+        scatter_kernel,
+        out_shape=jax.ShapeDtypeStruct(block, jnp.float32),
+        in_specs=vmem(1),
+        out_specs=vmem(1)[0],
+        scratch_shapes=[
+            pltpu.VMEM((2, UP, NY, *block), jnp.float32),
+            pltpu.VMEM((NY, *block), jnp.float32),
+            pltpu.VMEM((NY, *block), jnp.float32),
+            dma((NY,)), dma((NY,)), dma((2, UP, NY)), dma((2, UP, NY)),
+        ],
+        compiler_params=pltpu.CompilerParams(collective_id=number, has_side_effects=True),
+    )(sums)
+
+
+def hour_kernel(n, in_ref, out_ref, arrived, send_sem, recv_sem):
+    me = lax.axis_index("hour")
+    order = [n // 2] + [d for d in range(1, n) if d != n // 2]
+
+    def copy(d):
+        return remote(in_ref, arrived.at[d], send_sem.at[d], recv_sem.at[d], hour=lax.rem(me + d, n))
+
+    peers = [lax.rem(me + d, n) for d in order]
+    pl.semaphore_wait(pltpu.get_barrier_semaphore(), greet("hour", peers))
+    for d in order:
+        copy(d).start()
+    arrived[0] = in_ref[...]
+    for d in order:
+        copy(d).wait()
+    out_ref[...] = jnp.sum(arrived[...], axis=0)
+
+
+def hour_total(x, number):
+    n = lax.axis_size("hour")
+    dma = pltpu.SemaphoreType.DMA
+    return pl.pallas_call(
+        lambda *refs: hour_kernel(n, *refs),
+        out_shape=jax.ShapeDtypeStruct(x.shape, jnp.float32),
+        in_specs=vmem(1),
+        out_specs=vmem(1)[0],
+        scratch_shapes=[pltpu.VMEM((n, *x.shape), jnp.float32), dma((n,)), dma((n,))],
+        compiler_params=pltpu.CompilerParams(collective_id=number, has_side_effects=True),
+    )(x)
+
+
+def samp_kernel(in_ref, out_ref, first, middle, second, send_y, recv_y, send_z, recv_z):
+    me = lax.axis_index("samp")
+    z, y = me // NY, lax.rem(me, NY)
+    far_first = sorted(range(1, NZ), key=lambda d: -min(d, NZ - d))
+
+    def y_copy(d):
+        return remote(in_ref, first.at[d], send_y.at[d], recv_y.at[d], samp=at_place(z, y + d))
+
+    def z_copy(d):
+        return remote(middle, second.at[d], send_z.at[d], recv_z.at[d], samp=at_place(z + d, y))
+
+    peers = [at_place(z + d, y) for d in far_first] + [at_place(z, y + d) for d in (2, 1, 3)]
+    pl.semaphore_wait(pltpu.get_barrier_semaphore(), greet("samp", peers))
+    for d in (2, 1, 3):
+        y_copy(d).start()
+    first[0] = in_ref[...]
+    for d in (1, 3, 2):
+        y_copy(d).wait()
+    middle[...] = jnp.sum(first[...], axis=0)
+    for d in far_first:
+        z_copy(d).start()
+    second[0] = middle[...]
+    for d in far_first[::-1]:
+        z_copy(d).wait()
+    out_ref[...] = jnp.sum(second[...], axis=0)
+
+
+def samp_total(x, number):
+    dma = pltpu.SemaphoreType.DMA
+    return pl.pallas_call(
+        samp_kernel,
+        out_shape=jax.ShapeDtypeStruct(x.shape, jnp.float32),
+        in_specs=vmem(1),
+        out_specs=vmem(1)[0],
+        scratch_shapes=[
+            pltpu.VMEM((NY, *x.shape), jnp.float32),
+            pltpu.VMEM(x.shape, jnp.float32),
+            pltpu.VMEM((NZ, *x.shape), jnp.float32),
+            dma((NY,)), dma((NY,)), dma((NZ,)), dma((NZ,)),
+        ],
+        compiler_params=pltpu.CompilerParams(collective_id=number, has_side_effects=True),
+    )(x)
 
 
 def two_pieces(x, axis):
@@ -33,8 +315,8 @@
     def padded(rows):
         return jnp.pad(rows, ((0, PAD - per_owner), (0, 0)))
 
-    def backward(rows):
-        everyone = lax.all_gather(padded(rows), "samp", tiled=True)
+    def backward(rows, number):
+        everyone = everyone_of(padded(rows), number)
         square = jnp.sum(everyone * everyone)
         pieces = two_pieces(everyone, 1)
         spread = lax.dot_general(
@@ -42,15 +324,15 @@
         )
         spread = (spread[:row_width] + spread[row_width:]).reshape(use_count, hour_dev, samp_dev)
         partial = jnp.sum(wide * spread, axis=1)
-        extra = jnp.zeros((1, samp_dev), jnp.float32).at[0, 0].set(square)
-        total = lax.psum(jnp.concatenate([partial, extra], axis=0), "hour")
-        return total[:use_count], total[use_count, 0]
+        rest = jnp.full((8, 128), square)
+        total = hour_total(jnp.concatenate([partial.reshape(-1, 128), rest], axis=0), number + 1)
+        return total[:-8].reshape(use_count, samp_dev), total[-1, 0]
 
     def my_share(x):
         return lax.dynamic_slice_in_dim(x, hour_index * share_len, share_len, 1)
 
     gap_rows = load_gap.reshape(per_owner, row_width)
-    plain, gap_total = backward(gap_rows)
+    plain, gap_total = backward(gap_rows, 1)
     beta_one = jnp.sqrt(gap_total / space_count + epsilon)
     image = plain / beta_one
     weighted = (wide * image[:, None, :]).reshape(row_width, samp_dev)
@@ -60,16 +342,16 @@
     sums = (sums[:, :row_width] + sums[:, row_width:]).reshape(owners, PAD, row_width)
     mine = jnp.sum(image * image)
     row = jnp.arange(PAD, dtype=jnp.int32)[None, :, None]
-    sums = jnp.where(row == per_owner, mine, sums).reshape(owners * PAD, row_width)
-    owned = lax.psum_scatter(sums, "samp", scatter_dimension=0, tiled=True)
+    sums = jnp.where(row == per_owner, mine, sums)
+    owned = owned_of(sums, 5)
     alpha_one = jnp.sqrt(owned[per_owner, 0] / sample_count + epsilon)
     mismatch = owned[:per_owner] / alpha_one - (alpha_one / beta_one) * gap_rows
-    back, mismatch_total = backward(mismatch)
+    back, mismatch_total = backward(mismatch, 3)
     beta_two = jnp.sqrt(mismatch_total / space_count + epsilon)
     load_dir = mismatch / beta_two
     vector_one = image / alpha_one
     image_two = back / beta_two - beta_two * vector_one
-    second_total = lax.psum(jnp.sum(image_two * image_two), "samp")
+    second_total = samp_total(jnp.full((8, 128), jnp.sum(image_two * image_two)), 6)[0, 0]
     alpha_two = jnp.sqrt(second_total / sample_count + epsilon)
     rho_value = jnp.sqrt(alpha_one * alpha_one + beta_two * beta_two)
     cosine = alpha_one / rho_value

time: 1210 us -> 206 us (0.17)
  the two profiles are of different devices: /device:TPU:8 before, /device:TPU:1 now
where the time goes in v2:
time: 206 us; the launch traced here: 205 us
  Pallas kernels  153 us (74%)
  local copies, waits for them, and re-layouts  20.2 us (10%)
  matrix products  14.8 us (7%)
  other arithmetic  13.4 us (7%)
  between operations  3.9 us (2%)
    pallas_call x2, Pallas kernels, everyone_of(): pl.pallas_call(gather_kernel, out_shape=jax.ShapeDtypeStruct((count, *row...  67.7 us
    pallas_call x2, Pallas kernels, hour_total(): pl.pallas_call(lambda *refs: hour_kernel(n, *refs), out_shape=jax.ShapeDt...  39.2 us
    pallas_call x1, Pallas kernels, owned_of(): pl.pallas_call(scatter_kernel, out_shape=jax.ShapeDtypeStruct(block, jnp....  29.6 us
    pallas_call x1, Pallas kernels, samp_total(): pl.pallas_call(samp_kernel, out_shape=jax.ShapeDtypeStruct(x.shape, jnp.f...  15.9 us
    dot_general x2, matrix products, backward(): lax.dot_general(pieces, onehot, (((0,), (0,)), ((), ())), preferred_eleme...  9.88 us
    gather x1, local copies, waits for them, and re-layouts, local(): county = jnp.take(my_counties, slot_of_sample)  8.58 us
    reduce_sum x2, other arithmetic, backward(): square = jnp.sum(everyone * everyone)  5.13 us
    dot_general x1, matrix products, local(): lax.dot_general(onehot, two_pieces(weighted, 0), (((1,), (1,)), ((), ()))...  4.9 us

profile of v2, /device:TPU:1, one launch (start us, length us, event | category | flops | bytes accessed | tf_op | source)
XLA Modules:
  0.0 204.8 jit_solution(12433514740882777227)
XLA Ops:
  0.7 0.9 copy-done
  2.3 8.6 %gather_fusion = s32[2048]{0:T(1024)S(1)} fusion(s32[1024]{0:T(1024)S(1)} %bitcast.21, s32[2048]{0:T(1024)S(1)} %fusion.23), kind=kCustom, calls=%fused_computation | custom fusion | bytes 24576 | tf_op jit(solution)/shard_map/jit(_take)/gather | solution.py:309
  11.6 40.1 %shard_map.67 = f32[64,48,128]{2,1,0:T(8,128)} custom-call(f32[48,128]{1,0:T(8,128)} %pad.9.in_ref), custom_call_target="tpu_custom_call" | custom-call | tf_op jit(solution)/shard_map/pallas_call | solution.py:120
  51.8 2.5 %multiply_reduce_fusion.1 = f32[]{:T(128)} fusion(f32[64,48,128]{2,1,0:T(8,128)} %shard_map.67), kind=kLoop, calls=%fused_computation.22 | loop fusion | flops 786431 | bytes 1572868 | tf_op jit(solution)/shard_map/reduce_sum | solution.py:320
  54.6 4.9 %fusion.2 = f32[256,2048]{1,0:T(8,128)S(1)} fusion(s32[2048]{0:T(1024)S(1)} %fusion.21, bf16[3072,128]{1,0:T(8,128)(2,1)S(1)} %get-tuple-element.16, bf16[3072,128]{1,0:T(8,128)(2,1)S(1)} %get-tuple-element.15), kind=kOutput, calls=%fused_computation.4 | convolution fusion | flops 3230662656 | bytes 3678208 | tf_op jit(solution)/shard_map/dot_general | solution.py:322
  59.9 1.3 concatenate.19.refs_0_
  61.1 16.4 %shard_map.68 = f32[72,128]{1,0:T(8,128)} custom-call(f32[72,128]{1,0:T(8,128)} %concatenate.19.refs_0_), custom_call_target="tpu_custom_call" | custom-call | tf_op jit(solution)/shard_map/pallas_call | solution.py:238
  77.6 1.2 slice.42
  79.5 1.4 multiply_reduce_fusion.3
  81.1 4.9 %fusion.1 = f32[3072,256]{1,0:T(8,128)S(1)} fusion(s32[2048]{0:T(1024)S(1)} %fusion.21, bf16[128,2048]{1,0:T(8,128)(2,1)S(1)} %get-tuple-element.18, bf16[128,2048]{1,0:T(8,128)(2,1)S(1)} %get-tuple-element.17), kind=kOutput, calls=%fused_computation.3 | convolution fusion | flops 3229614080 | bytes 4202496 | tf_op jit(solution)/shard_map/dot_general | solution.py:339
  86.2 2.0 broadcast_select_fusion.in_ref
  88.2 29.6 %shard_map.69 = f32[48,128]{1,0:T(8,128)} custom-call(f32[64,48,128]{2,1,0:T(8,128)} %broadcast_select_fusion.in_ref), custom_call_target="tpu_custom_call" | custom-call | tf_op jit(solution)/shard_map/pallas_call | solution.py:203
  117.8 1.2 slice.45
  119.7 0.7 multiply_subtract_fusion
  121.1 27.6 %shard_map.70 = f32[64,48,128]{2,1,0:T(8,128)} custom-call(f32[48,128]{1,0:T(8,128)} %pad.10.in_ref), custom_call_target="tpu_custom_call" | custom-call | tf_op jit(solution)/shard_map/pallas_call | solution.py:120
  148.7 2.6 %multiply_reduce_fusion = f32[]{:T(128)} fusion(f32[64,48,128]{2,1,0:T(8,128)} %shard_map.70), kind=kLoop, calls=%fused_computation.21 | loop fusion | flops 786431 | bytes 1572868 | tf_op jit(solution)/shard_map/reduce_sum | solution.py:320
  151.6 4.9 %fusion = f32[256,2048]{1,0:T(8,128)S(1)} fusion(s32[2048]{0:T(1024)S(1)} %fusion.21, bf16[3072,128]{1,0:T(8,128)(2,1)S(1)} %get-tuple-element.14, bf16[3072,128]{1,0:T(8,128)(2,1)S(1)} %get-tuple-element.13), kind=kOutput, calls=%fused_computation.2 | convolution fusion | flops 3230662656 | bytes 3678208 | tf_op jit(solution)/shard_map/dot_general | solution.py:322
  156.8 1.2 concatenate.22.refs_0_
  158.0 22.8 %shard_map.71 = f32[72,128]{1,0:T(8,128)} custom-call(f32[72,128]{1,0:T(8,128)} %concatenate.22.refs_0_), custom_call_target="tpu_custom_call" | custom-call | tf_op jit(solution)/shard_map/pallas_call | solution.py:238
  180.8 1.2 slice.49
  182.9 1.4 multiply_reduce_fusion.2
  184.3 1.2 broadcast_in_dim.33.in_ref
  185.5 15.9 %shard_map.72 = f32[8,128]{1,0:T(8,128)} custom-call(f32[8,128]{1,0:T(8,128)} %broadcast_in_dim.33.in_ref), custom_call_target="tpu_custom_call" | custom-call | tf_op jit(solution)/shard_map/pallas_call | solution.py:277
  201.5 1.2 slice.51
  (35 shorter events, 5.0 us)
Async XLA Ops:
  0.6 1.0 copy-start
  2.3 8.6 %copy-start.6 = (s32[2048]{0:T(1024)S(1)}, s32[2048]{0:T(1024)}, u32[]{:S(2)}) copy-start(s32[2048]{0:T(1024)} %param.6) | copy-start | bytes 24580
  2.3 8.6 %copy-start.5 = (f32[47,4,32]{0,2,1:T(8,128)S(1)}, f32[47,4,32]{0,2,1:T(8,128)}, u32[]{:S(2)}) copy-start(f32[47,4,32]{0,2,1:T(8,128)} %param.4) | copy-start | bytes 72196
  51.8 2.5 %copy-start.1 = (f32[64,48,128]{2,1,0:T(8,128)S(1)}, f32[64,48,128]{2,1,0:T(8,128)}, u32[]{:S(2)}) copy-start(f32[64,48,128]{2,1,0:T(8,128)} %shard_map.67) | copy-start | bytes 4718596
  54.6 5.0 %copy-start.3 = (bf16[4,32,2048]{2,1,0:T(8,128)(2,1)S(1)}, bf16[4,32,2048]{2,1,0:T(8,128)(2,1)}, u32[]{:S(2)}) copy-start(bf16[4,32,2048]{2,1,0:T(8,128)(2,1)} %param.5) | copy-start | bytes 1572868
  148.7 2.6 %copy-start.2 = (f32[64,48,128]{2,1,0:T(8,128)S(1)}, f32[64,48,128]{2,1,0:T(8,128)}, u32[]{:S(2)}) copy-start(f32[64,48,128]{2,1,0:T(8,128)} %shard_map.70) | copy-start | bytes 4718596
  156.5 26.4 %copy-start.4 = (f32[72,128]{1,0:T(8,128)S(1)}, f32[72,128]{1,0:T(8,128)}, u32[]{:S(2)}) copy-start(f32[72,128]{1,0:T(8,128)} %shard_map.68) | copy-start | bytes 110596

commit v3 on v2

--- a/solution.py
+++ b/solution.py
@@ -7,6 +7,7 @@
 
 epsilon = 1e-06
 PAD = 48
+HALF = 24
 MESH = pl.DeviceIdType.MESH
 NY = 4
 NZ = 16
@@ -36,41 +37,80 @@
     return [at_place(z, y + d) for d in range(1, NY)] + [at_place(z + 1, y), at_place(z - 1, y)]
 
 
-def gather_body(in_ref, out_ref, send_y, recv_y, send_z, recv_z):
+def gather_body(in_ref, out_ref, send_y, recv_y, send_z, recv_z, send_t, recv_t, send_u, recv_u):
     me = lax.axis_index("samp")
     z, y = me // NY, lax.rem(me, NY)
+    top, bottom = pl.ds(0, HALF), pl.ds(HALF, PAD - HALF)
 
     def y_copy(d):
-        return remote(in_ref, out_ref.at[me], send_y.at[d], recv_y.at[d], samp=at_place(z, y + d))
+        return remote(
+            in_ref.at[top], out_ref.at[me, top], send_y.at[d], recv_y.at[d], samp=at_place(z, y + d)
+        )
 
     def y_arrival(d):
-        slot = out_ref.at[at_place(z, y - d)]
+        slot = out_ref.at[at_place(z, y - d), top]
         return remote(slot, slot, send_y.at[d], recv_y.at[d], samp=at_place(z, y + d))
 
     def z_copy(way, k, j, own=False):
         step = 1 - 2 * way
-        slot = out_ref.at[at_place(z - step * k, y - j)]
-        return remote(
-            in_ref if own else slot, slot, send_z.at[way, k, j], recv_z.at[way, k, j],
+        slot = out_ref.at[at_place(z - step * k, y - j), top]
+        return remote(
+            in_ref.at[top] if own else slot, slot, send_z.at[way, k, j], recv_z.at[way, k, j],
             samp=at_place(z + step, y),
         )
 
     def z_arrival(way, k, j):
         step = 1 - 2 * way
-        slot = out_ref.at[at_place(z - step * (k + 1), y - j)]
+        slot = out_ref.at[at_place(z - step * (k + 1), y - j), top]
         return remote(slot, slot, send_z.at[way, k, j], recv_z.at[way, k, j], samp=at_place(z + step, y))
 
-    z_copy(0, 0, 0, True).start()
-    z_copy(1, 0, 0, True).start()
+    def t_copy(way, k, own=False):
+        step = 1 - 2 * way
+        slot = out_ref.at[at_place(z - step * k, y), bottom]
+        return remote(
+            in_ref.at[bottom] if own else slot, slot, send_t.at[way, k], recv_t.at[way, k],
+            samp=at_place(z + step, y),
+        )
+
+    def t_arrival(way, k):
+        step = 1 - 2 * way
+        slot = out_ref.at[at_place(z - step * (k + 1), y), bottom]
+        return remote(slot, slot, send_t.at[way, k], recv_t.at[way, k], samp=at_place(z + step, y))
+
+    def u_copy(off, d, own=False):
+        slot = out_ref.at[at_place(z + off, y), bottom]
+        return remote(
+            in_ref.at[bottom] if own else slot, slot, send_u.at[off, d], recv_u.at[off, d],
+            samp=at_place(z, y + d),
+        )
+
+    def u_arrival(off, d):
+        slot = out_ref.at[at_place(z + off, y - d), bottom]
+        return remote(slot, slot, send_u.at[off, d], recv_u.at[off, d], samp=at_place(z, y + d))
+
+    for way in (0, 1):
+        t_copy(way, 0, True).start()
+        z_copy(way, 0, 0, True).start()
     for d in (2, 1, 3):
         y_copy(d).start()
+    for d in (2, 1, 3):
+        u_copy(0, d, True).start()
     out_ref[pl.ds(me, 1)] = in_ref[...][None]
     for j in (1, 3, 2):
         y_arrival(j).wait_recv()
-        z_copy(0, 0, j).start()
-        z_copy(1, 0, j).start()
+        for way in (0, 1):
+            z_copy(way, 0, j).start()
+
+    def fan_out(way, k):
+        off = NZ - 1 - k if way == 0 else k + 1
+        for d in (2, 1, 3):
+            u_copy(off, d).start()
 
     def hop(k, carry):
+        for way in (0, 1):
+            t_arrival(way, k - 1).wait_recv()
+            t_copy(way, k).start()
+            fan_out(way, k - 1)
         for j in (0, 1, 3, 2):
             for way in (0, 1):
                 z_arrival(way, k - 1, j).wait_recv()
@@ -78,35 +118,54 @@
         return carry
 
     lax.fori_loop(1, DOWN, hop, 0)
+    t_arrival(0, UP - 2).wait_recv()
+    t_copy(0, UP - 1).start()
+    fan_out(0, UP - 2)
+    t_arrival(1, DOWN - 1).wait_recv()
+    fan_out(1, DOWN - 1)
     for j in (0, 1, 3, 2):
         z_arrival(0, UP - 2, j).wait_recv()
         z_copy(0, UP - 1, j).start()
         z_arrival(1, DOWN - 1, j).wait_recv()
+    t_arrival(0, UP - 1).wait_recv()
+    fan_out(0, UP - 1)
     for d in (2, 1, 3):
         y_copy(d).wait_send()
-    z_copy(0, 0, 0, True).wait_send()
-    z_copy(1, 0, 0, True).wait_send()
-    for j in (1, 3, 2):
-        z_copy(0, 0, j).wait_send()
-        z_copy(1, 0, j).wait_send()
+        u_copy(0, d, True).wait_send()
+        u_arrival(0, d).wait_recv()
+    for way in (0, 1):
+        t_copy(way, 0, True).wait_send()
+        z_copy(way, 0, 0, True).wait_send()
+        for j in (1, 3, 2):
+            z_copy(way, 0, j).wait_send()
 
     def drain(k, carry):
-        for j in (0, 1, 3, 2):
-            for way in (0, 1):
+        for way in (0, 1):
+            t_copy(way, k).wait_send()
+            for j in (0, 1, 3, 2):
                 z_copy(way, k, j).wait_send()
         return carry
 
     lax.fori_loop(1, DOWN, drain, 0)
+
+    def drain_u(off, carry):
+        for d in (2, 1, 3):
+            u_copy(off, d).wait_send()
+            u_arrival(off, d).wait_recv()
+        return carry
+
+    lax.fori_loop(1, NZ, drain_u, 0)
+    t_copy(0, UP - 1).wait_send()
     for j in (0, 1, 3, 2):
         z_copy(0, UP - 1, j).wait_send()
         z_arrival(0, UP - 1, j).wait_recv()
 
 
-def gather_kernel(in_ref, out_ref, got, send_y, recv_y, send_z, recv_z):
+def gather_kernel(in_ref, out_ref, got, *sems):
     me = lax.axis_index("samp")
     z, y = me // NY, lax.rem(me, NY)
     pl.semaphore_wait(pltpu.get_barrier_semaphore(), greet("samp", near_peers(z, y)))
-    gather_body(in_ref, got, send_y, recv_y, send_z, recv_z)
+    gather_body(in_ref, got, *sems)
     out_ref[...] = got[...]
 
 
@@ -125,80 +184,150 @@
         scratch_shapes=[
             pltpu.VMEM((count, *rows.shape), jnp.float32),
             dma((NY,)), dma((NY,)), dma((2, UP, NY)), dma((2, UP, NY)),
+            dma((2, UP)), dma((2, UP)), dma((NZ, NY)), dma((NZ, NY)),
         ],
         compiler_params=pltpu.CompilerParams(collective_id=number, has_side_effects=True),
     )(rows).reshape(count * rows.shape[0], rows.shape[1])
 
 
-def scatter_kernel(in_ref, out_ref, held, total, arrived, send_y, recv_y, send_z, recv_z):
+def scatter_body(
+    in_ref, out_ref, held, total, arrived, crossed, chain, first,
+    send_y, recv_y, send_z, recv_z, send_t, recv_t, send_u, recv_u,
+):
     me = lax.axis_index("samp")
     z, y = me // NY, lax.rem(me, NY)
+    top, bottom = pl.ds(0, HALF), pl.ds(HALF, PAD - HALF)
     order = (2, 1, 3, 0)
 
+    def target(way, k):
+        return (UP - k) if way == 0 else (NZ - DOWN + k)
+
     def z_copy(way, k, j, own=False):
-        step = 1 - 2 * way
-        far = (UP, DOWN)[way] - k
-        src = in_ref.at[at_place(z + step * far, y + j)] if own else held.at[way, k - 1, j]
+        src = in_ref.at[at_place(z + target(way, k), y + j), top] if own else held.at[way, k - 1, j]
         return remote(
             src, held.at[way, k, j], send_z.at[way, k, j], recv_z.at[way, k, j],
-            samp=at_place(z + step, y),
+            samp=at_place(z + 1 - 2 * way, y),
         )
 
     def z_arrival(way, k, j):
-        step = 1 - 2 * way
         slot = held.at[way, k, j]
-        return remote(slot, slot, send_z.at[way, k, j], recv_z.at[way, k, j], samp=at_place(z + step, y))
+        return remote(
+            slot, slot, send_z.at[way, k, j], recv_z.at[way, k, j], samp=at_place(z + 1 - 2 * way, y)
+        )
 
     def add_own(way, k, j):
-        step = 1 - 2 * way
-        far = (UP, DOWN)[way] - k
         z_arrival(way, k - 1, j).wait_recv()
-        held[way, k - 1, j] = held[way, k - 1, j] + in_ref[at_place(z + step * far, y + j)]
+        held[way, k - 1, j] = held[way, k - 1, j] + in_ref[at_place(z + target(way, k), y + j), top]
         z_copy(way, k, j).start()
+
+    def u_copy(off, d):
+        return remote(
+            in_ref.at[at_place(z + off, y + d), bottom], crossed.at[off, d],
+            send_u.at[off, d], recv_u.at[off, d], samp=at_place(z, y + d),
+        )
+
+    def crossed_sum(off):
+        for d in (1, 3, 2):
+            u_copy(off, d).wait_recv()
+        own = in_ref[at_place(z + off, y), bottom]
+        return own + crossed[off, 1] + crossed[off, 2] + crossed[off, 3]
+
+    def t_copy(way, k, own=False):
+        return remote(
+            first.at[way] if own else chain.at[way, k - 1], chain.at[way, k],
+            send_t.at[way, k], recv_t.at[way, k], samp=at_place(z + 1 - 2 * way, y),
+        )
+
+    def t_arrival(way, k):
+        slot = chain.at[way, k]
+        return remote(slot, slot, send_t.at[way, k], recv_t.at[way, k], samp=at_place(z + 1 - 2 * way, y))
+
+    def add_crossed(way, k):
+        mine = crossed_sum(target(way, k))
+        t_arrival(way, k - 1).wait_recv()
+        chain[way, k - 1] = chain[way, k - 1] + mine
+        t_copy(way, k).start()
 
     def y_copy(d):
         return remote(total.at[d], arrived.at[d], send_y.at[d], recv_y.at[d], samp=at_place(z, y + d))
 
-    pl.semaphore_wait(pltpu.get_barrier_semaphore(), greet("samp", near_peers(z, y)))
+    def launch(k, carry):
+        for way in (0, 1):
+            for d in (2, 1, 3):
+                u_copy(target(way, k), d).start()
+        return carry
+
+    launch(0, 0)
     for j in order:
         for way in (0, 1):
             z_copy(way, 0, j, True).start()
+    lax.fori_loop(1, DOWN, launch, 0)
+    for off in (1, 0):
+        for d in (2, 1, 3):
+            u_copy(off, d).start()
+    for way in (0, 1):
+        first[way] = crossed_sum(target(way, 0))
+        t_copy(way, 0, True).start()
 
     def hop(k, carry):
         for j in order:
             for way in (0, 1):
                 add_own(way, k, j)
+        for way in (0, 1):
+            add_crossed(way, k)
         return carry
 
     lax.fori_loop(1, DOWN, hop, 0)
     for j in order:
         add_own(0, UP - 1, j)
+    add_crossed(0, UP - 1)
     for j in order:
         z_arrival(1, DOWN - 1, j).wait_recv()
         z_arrival(0, UP - 1, j).wait_recv()
-        total[j] = held[0, UP - 1, j] + held[1, DOWN - 1, j] + in_ref[at_place(z, y + j)]
+        total[j] = held[0, UP - 1, j] + held[1, DOWN - 1, j] + in_ref[at_place(z, y + j), top]
         if j:
             y_copy(j).start()
+    mine = crossed_sum(0)
+    t_arrival(1, DOWN - 1).wait_recv()
+    t_arrival(0, UP - 1).wait_recv()
+    out_ref[bottom] = mine + chain[0, UP - 1] + chain[1, DOWN - 1]
 
     def drain(k, carry):
+        for way in (0, 1):
+            t_copy(way, k).wait_send()
+            for j in order:
+                z_copy(way, k, j).wait_send()
+        return carry
+
+    def drain_u(off, carry):
+        for d in (2, 1, 3):
+            u_copy(off, d).wait_send()
+        return carry
+
+    for way in (0, 1):
+        t_copy(way, 0, True).wait_send()
         for j in order:
-            for way in (0, 1):
-                z_copy(way, k, j).wait_send()
-        return carry
-
-    for j in order:
-        for way in (0, 1):
             z_copy(way, 0, j, True).wait_send()
     lax.fori_loop(1, DOWN, drain, 0)
+    lax.fori_loop(0, NZ, drain_u, 0)
+    t_copy(0, UP - 1).wait_send()
     for j in order:
         z_copy(0, UP - 1, j).wait_send()
     for d in (1, 3, 2):
         y_copy(d).wait()
-    out_ref[...] = total[0] + arrived[1] + arrived[2] + arrived[3]
+    out_ref[top] = total[0] + arrived[1] + arrived[2] + arrived[3]
+
+
+def scatter_kernel(in_ref, out_ref, *scratch):
+    me = lax.axis_index("samp")
+    z, y = me // NY, lax.rem(me, NY)
+    pl.semaphore_wait(pltpu.get_barrier_semaphore(), greet("samp", near_peers(z, y)))
+    scatter_body(in_ref, out_ref, *scratch)
 
 
 def owned_of(sums, number):
     block = sums.shape[1:]
+    upper, lower = (HALF, block[1]), (PAD - HALF, block[1])
     dma = pltpu.SemaphoreType.DMA
     return pl.pallas_call(
         scatter_kernel,
@@ -206,10 +335,14 @@
         in_specs=vmem(1),
         out_specs=vmem(1)[0],
         scratch_shapes=[
-            pltpu.VMEM((2, UP, NY, *block), jnp.float32),
-            pltpu.VMEM((NY, *block), jnp.float32),
-            pltpu.VMEM((NY, *block), jnp.float32),
+            pltpu.VMEM((2, UP, NY, *upper), jnp.float32),
+            pltpu.VMEM((NY, *upper), jnp.float32),
+            pltpu.VMEM((NY, *upper), jnp.float32),
+            pltpu.VMEM((NZ, NY, *lower), jnp.float32),
+            pltpu.VMEM((2, UP, *lower), jnp.float32),
+            pltpu.VMEM((2, *lower), jnp.float32),
             dma((NY,)), dma((NY,)), dma((2, UP, NY)), dma((2, UP, NY)),
+            dma((2, UP)), dma((2, UP)), dma((NZ, NY)), dma((NZ, NY)),
         ],
         compiler_params=pltpu.CompilerParams(collective_id=number, has_side_effects=True),
     )(sums)
@@ -306,7 +439,10 @@
     space_count = float(per_owner * owners * row_width * hour_count)
     sample_count = float(use_count * samp_dev * owners)
     my_counties = lax.dynamic_index_in_dim(slot_county, owner_index, 0, keepdims=False)
-    county = jnp.take(my_counties, slot_of_sample)
+    slots = jnp.arange(slot_county.shape[1], dtype=jnp.int32)
+    county = jnp.sum(
+        jnp.where(slots[:, None] == slot_of_sample[None, :], my_counties[:, None], 0), axis=0
+    )
     place = county // per_owner * PAD + county % per_owner
     places = jnp.arange(owners * PAD, dtype=jnp.int32)
     onehot = (places[:, None] == place[None, :]).astype(jnp.bfloat16)

time: 206 us -> 204 us (level)
  local copies, waits for them, and re-layouts: 20.2 us -> 12.5 us
  Pallas kernels: 153 us -> 157 us
    gather x1 -> x0, local copies, waits for them, and re-layouts: 8.58 us -> none  [local(): county = jnp.take(my_counties, slot_of_sample)]
where the time goes in v3:
time: 204 us; the launch traced here: 203 us
  Pallas kernels  157 us (77%)
  matrix products  14.8 us (7%)
  other arithmetic  14.5 us (7%)
  local copies, waits for them, and re-layouts  12.5 us (6%)
  between operations  3.88 us (2%)
    pallas_call x2, Pallas kernels, everyone_of(): pl.pallas_call(gather_kernel, out_shape=jax.ShapeDtypeStruct((count, *row...  69.7 us
    pallas_call x2, Pallas kernels, hour_total(): pl.pallas_call(lambda *refs: hour_kernel(n, *refs), out_shape=jax.ShapeDt...  40.7 us
    pallas_call x1, Pallas kernels, owned_of(): pl.pallas_call(scatter_kernel, out_shape=jax.ShapeDtypeStruct(block, jnp....  30.1 us
    pallas_call x1, Pallas kernels, samp_total(): pl.pallas_call(samp_kernel, out_shape=jax.ShapeDtypeStruct(x.shape, jnp.f...  16.5 us
    dot_general x2, matrix products, backward(): lax.dot_general(pieces, onehot, (((0,), (0,)), ((), ())), preferred_eleme...  9.87 us
    reduce_sum x2, other arithmetic, backward(): square = jnp.sum(everyone * everyone)  5.13 us
    dot_general x1, matrix products, local(): lax.dot_general(onehot, two_pieces(weighted, 0), (((1,), (1,)), ((), ()))...  4.9 us

profile of v3, /device:TPU:1, one launch (start us, length us, event | category | flops | bytes accessed | tf_op | source)
XLA Modules:
  0.0 202.6 jit_solution(15382246915877388713)
XLA Ops:
  0.7 0.9 copy-done
  1.6 1.8 select_reduce_fusion
  3.4 0.9 copy.13
  4.9 40.1 %shard_map.67 = f32[64,48,128]{2,1,0:T(8,128)} custom-call(f32[48,128]{1,0:T(8,128)} %pad.9.in_ref), custom_call_target="tpu_custom_call" | custom-call | tf_op jit(solution)/shard_map/pallas_call | solution.py:179
  45.1 2.5 %multiply_reduce_fusion.1 = f32[]{:T(128)} fusion(f32[64,48,128]{2,1,0:T(8,128)} %shard_map.67), kind=kLoop, calls=%fused_computation.23 | loop fusion | flops 786431 | bytes 1572868 | tf_op jit(solution)/shard_map/reduce_sum | solution.py:456
  47.9 4.9 %fusion.2 = f32[256,2048]{1,0:T(8,128)S(1)} fusion(s32[2048]{0:T(1024)S(1)} %fusion.21, bf16[3072,128]{1,0:T(8,128)(2,1)S(1)} %get-tuple-element.19, bf16[3072,128]{1,0:T(8,128)(2,1)S(1)} %get-tuple-element.18), kind=kOutput, calls=%fused_computation.3 | convolution fusion | flops 3230662656 | bytes 3678208 | tf_op jit(solution)/shard_map/dot_general | solution.py:458
  53.1 1.3 concatenate.19.refs_0_
  54.4 17.1 %shard_map.68 = f32[72,128]{1,0:T(8,128)} custom-call(f32[72,128]{1,0:T(8,128)} %concatenate.19.refs_0_), custom_call_target="tpu_custom_call" | custom-call | tf_op jit(solution)/shard_map/pallas_call | solution.py:371
  71.6 1.2 slice.42
  73.4 1.4 multiply_reduce_fusion.3
  75.1 4.9 %fusion.1 = f32[3072,256]{1,0:T(8,128)S(1)} fusion(s32[2048]{0:T(1024)S(1)} %fusion.21, bf16[128,2048]{1,0:T(8,128)(2,1)S(1)} %get-tuple-element.21, bf16[128,2048]{1,0:T(8,128)(2,1)S(1)} %get-tuple-element.20), kind=kOutput, calls=%fused_computation.2 | convolution fusion | flops 3229614080 | bytes 4202496 | tf_op jit(solution)/shard_map/dot_general | solution.py:475
  80.2 2.0 broadcast_select_fusion.in_ref
  82.1 30.1 %shard_map.69 = f32[48,128]{1,0:T(8,128)} custom-call(f32[64,48,128]{2,1,0:T(8,128)} %broadcast_select_fusion.in_ref), custom_call_target="tpu_custom_call" | custom-call | tf_op jit(solution)/shard_map/pallas_call | solution.py:332
  112.3 1.2 slice.45
  115.5 29.5 %shard_map.70 = f32[64,48,128]{2,1,0:T(8,128)} custom-call(f32[48,128]{1,0:T(8,128)} %pad.10.in_ref), custom_call_target="tpu_custom_call" | custom-call | tf_op jit(solution)/shard_map/pallas_call | solution.py:179
  145.1 2.6 %multiply_reduce_fusion = f32[]{:T(128)} fusion(f32[64,48,128]{2,1,0:T(8,128)} %shard_map.70), kind=kLoop, calls=%fused_computation.22 | loop fusion | flops 786431 | bytes 1572868 | tf_op jit(solution)/shard_map/reduce_sum | solution.py:456
  148.0 4.9 %fusion = f32[256,2048]{1,0:T(8,128)S(1)} fusion(s32[2048]{0:T(1024)S(1)} %fusion.21, bf16[3072,128]{1,0:T(8,128)(2,1)S(1)} %get-tuple-element.17, bf16[3072,128]{1,0:T(8,128)(2,1)S(1)} %get-tuple-element.16), kind=kOutput, calls=%fused_computation.1 | convolution fusion | flops 3230662656 | bytes 3678208 | tf_op jit(solution)/shard_map/dot_general | solution.py:458
  153.2 1.2 concatenate.22.refs_0_
  154.5 23.6 %shard_map.71 = f32[72,128]{1,0:T(8,128)} custom-call(f32[72,128]{1,0:T(8,128)} %concatenate.22.refs_0_), custom_call_target="tpu_custom_call" | custom-call | tf_op jit(solution)/shard_map/pallas_call | solution.py:371
  178.0 1.2 slice.49
  180.1 1.4 multiply_reduce_fusion.2
  181.5 1.2 broadcast_in_dim.43.in_ref
  182.8 16.5 %shard_map.72 = f32[8,128]{1,0:T(8,128)} custom-call(f32[8,128]{1,0:T(8,128)} %broadcast_in_dim.43.in_ref), custom_call_target="tpu_custom_call" | custom-call | tf_op jit(solution)/shard_map/pallas_call | solution.py:410
  199.3 1.2 slice.51
  (30 shorter events, 4.9 us)
Async XLA Ops:
  0.6 1.0 copy-start
  45.1 2.5 %copy-start.1 = (f32[64,48,128]{2,1,0:T(8,128)S(1)}, f32[64,48,128]{2,1,0:T(8,128)}, u32[]{:S(2)}) copy-start(f32[64,48,128]{2,1,0:T(8,128)} %shard_map.67) | copy-start | bytes 4718596
  47.9 4.9 %copy-start.3 = (bf16[4,32,2048]{2,1,0:T(8,128)(2,1)S(1)}, bf16[4,32,2048]{2,1,0:T(8,128)(2,1)}, u32[]{:S(2)}) copy-start(bf16[4,32,2048]{2,1,0:T(8,128)(2,1)} %param.5) | copy-start | bytes 1572868
  145.1 2.6 %copy-start.2 = (f32[64,48,128]{2,1,0:T(8,128)S(1)}, f32[64,48,128]{2,1,0:T(8,128)}, u32[]{:S(2)}) copy-start(f32[64,48,128]{2,1,0:T(8,128)} %shard_map.70) | copy-start | bytes 4718596
  152.9 27.2 %copy-start.4 = (f32[72,128]{1,0:T(8,128)S(1)}, f32[72,128]{1,0:T(8,128)}, u32[]{:S(2)}) copy-start(f32[72,128]{1,0:T(8,128)} %shard_map.68) | copy-start | bytes 110596

commit v4 on v2

--- a/solution.py
+++ b/solution.py
@@ -7,6 +7,8 @@
 
 epsilon = 1e-06
 PAD = 48
+HALF = 24
+GROUPS = 4
 MESH = pl.DeviceIdType.MESH
 NY = 4
 NZ = 16
@@ -36,77 +38,85 @@
     return [at_place(z, y + d) for d in range(1, NY)] + [at_place(z + 1, y), at_place(z - 1, y)]
 
 
-def gather_body(in_ref, out_ref, send_y, recv_y, send_z, recv_z):
+def gather_body(in_ref, out_ref, send_y, recv_y, send_z, recv_z, send_t, recv_t, send_u, recv_u):
     me = lax.axis_index("samp")
     z, y = me // NY, lax.rem(me, NY)
+    side = NY * NZ
 
     def y_copy(d):
-        return remote(in_ref, out_ref.at[me], send_y.at[d], recv_y.at[d], samp=at_place(z, y + d))
-
-    def y_arrival(d):
-        slot = out_ref.at[at_place(z, y - d)]
-        return remote(slot, slot, send_y.at[d], recv_y.at[d], samp=at_place(z, y + d))
-
-    def z_copy(way, k, j, own=False):
-        step = 1 - 2 * way
-        slot = out_ref.at[at_place(z - step * k, y - j)]
-        return remote(
-            in_ref if own else slot, slot, send_z.at[way, k, j], recv_z.at[way, k, j],
-            samp=at_place(z + step, y),
-        )
-
-    def z_arrival(way, k, j):
-        step = 1 - 2 * way
-        slot = out_ref.at[at_place(z - step * (k + 1), y - j)]
-        return remote(slot, slot, send_z.at[way, k, j], recv_z.at[way, k, j], samp=at_place(z + step, y))
-
-    z_copy(0, 0, 0, True).start()
-    z_copy(1, 0, 0, True).start()
+        return remote(
+            in_ref.at[pl.ds(0, 1)], out_ref.at[pl.ds(NY - d, 1)], send_y.at[d], recv_y.at[d],
+            samp=at_place(z, y + d),
+        )
+
+    def places(way, k):
+        return ((NZ - k) % NZ, NZ - k - 1) if way == 0 else (k, k + 1)
+
+    def z_copy(way, k):
+        here, there = places(way, k)
+        return remote(
+            out_ref.at[pl.ds(NY * here, NY)], out_ref.at[pl.ds(NY * there, NY)],
+            send_z.at[way, k], recv_z.at[way, k], samp=at_place(z + 1 - 2 * way, y),
+        )
+
+    def t_copy(way, k):
+        here, there = places(way, k)
+        src = in_ref.at[pl.ds(1, 1)] if k == 0 else out_ref.at[pl.ds(side + here, 1)]
+        return remote(
+            src, out_ref.at[pl.ds(side + there, 1)],
+            send_t.at[way, k], recv_t.at[way, k], samp=at_place(z + 1 - 2 * way, y),
+        )
+
+    def u_copy(group, d):
+        size = NZ // GROUPS
+        return remote(
+            out_ref.at[pl.ds(side + group * size, size)],
+            out_ref.at[pl.ds(side + (NY - d) * NZ + group * size, size)],
+            send_u.at[group, d], recv_u.at[group, d], samp=at_place(z, y + d),
+        )
+
+    steps = [(way, k) for k in range(UP) for way in (0, 1) if k < (UP, DOWN)[way]]
+    for way in (0, 1):
+        t_copy(way, 0).start()
     for d in (2, 1, 3):
         y_copy(d).start()
-    out_ref[pl.ds(me, 1)] = in_ref[...][None]
-    for j in (1, 3, 2):
-        y_arrival(j).wait_recv()
-        z_copy(0, 0, j).start()
-        z_copy(1, 0, j).start()
-
-    def hop(k, carry):
-        for j in (0, 1, 3, 2):
-            for way in (0, 1):
-                z_arrival(way, k - 1, j).wait_recv()
-                z_copy(way, k, j).start()
-        return carry
-
-    lax.fori_loop(1, DOWN, hop, 0)
-    for j in (0, 1, 3, 2):
-        z_arrival(0, UP - 2, j).wait_recv()
-        z_copy(0, UP - 1, j).start()
-        z_arrival(1, DOWN - 1, j).wait_recv()
+    out_ref[pl.ds(0, 1)] = in_ref[pl.ds(0, 1)]
+    out_ref[pl.ds(side, 1)] = in_ref[pl.ds(1, 1)]
+    for d in (1, 3, 2):
+        y_copy(d).wait_recv()
+    for way in (0, 1):
+        z_copy(way, 0).start()
+    landed = {0}
+    sent = set()
+    for way, k in steps:
+        t_copy(way, k).wait_recv()
+        landed.add(places(way, k)[1])
+        if (way, k + 1) in steps:
+            t_copy(way, k + 1).start()
+        for group in range(GROUPS):
+            size = NZ // GROUPS
+            if group not in sent and landed.issuperset(range(group * size, group * size + size)):
+                sent.add(group)
+                for d in (2, 1, 3):
+                    u_copy(group, d).start()
+        z_copy(way, k).wait_recv()
+        if (way, k + 1) in steps:
+            z_copy(way, k + 1).start()
     for d in (2, 1, 3):
         y_copy(d).wait_send()
-    z_copy(0, 0, 0, True).wait_send()
-    z_copy(1, 0, 0, True).wait_send()
-    for j in (1, 3, 2):
-        z_copy(0, 0, j).wait_send()
-        z_copy(1, 0, j).wait_send()
-
-    def drain(k, carry):
-        for j in (0, 1, 3, 2):
-            for way in (0, 1):
-                z_copy(way, k, j).wait_send()
-        return carry
-
-    lax.fori_loop(1, DOWN, drain, 0)
-    for j in (0, 1, 3, 2):
-        z_copy(0, UP - 1, j).wait_send()
-        z_arrival(0, UP - 1, j).wait_recv()
-
-
-def gather_kernel(in_ref, out_ref, got, send_y, recv_y, send_z, recv_z):
+    for way, k in steps:
+        t_copy(way, k).wait_send()
+        z_copy(way, k).wait_send()
+    for group in range(GROUPS):
+        for d in (2, 1, 3):
+            u_copy(group, d).wait()
+
+
+def gather_kernel(in_ref, out_ref, got, *sems):
     me = lax.axis_index("samp")
     z, y = me // NY, lax.rem(me, NY)
     pl.semaphore_wait(pltpu.get_barrier_semaphore(), greet("samp", near_peers(z, y)))
-    gather_body(in_ref, got, send_y, recv_y, send_z, recv_z)
+    gather_body(in_ref, got, *sems)
     out_ref[...] = got[...]
 
 
@@ -115,86 +125,113 @@
 
 
 def everyone_of(rows, number):
-    count = NY * NZ
+    whole = (2 * NY * NZ, HALF, rows.shape[1])
     dma = pltpu.SemaphoreType.DMA
     return pl.pallas_call(
         gather_kernel,
-        out_shape=jax.ShapeDtypeStruct((count, *rows.shape), jnp.float32),
+        out_shape=jax.ShapeDtypeStruct(whole, jnp.float32),
         in_specs=vmem(1),
         out_specs=vmem(1)[0],
         scratch_shapes=[
-            pltpu.VMEM((count, *rows.shape), jnp.float32),
-            dma((NY,)), dma((NY,)), dma((2, UP, NY)), dma((2, UP, NY)),
+            pltpu.VMEM(whole, jnp.float32),
+            dma((NY,)), dma((NY,)), dma((2, UP)), dma((2, UP)),
+            dma((2, UP)), dma((2, UP)), dma((GROUPS, NY)), dma((GROUPS, NY)),
         ],
         compiler_params=pltpu.CompilerParams(collective_id=number, has_side_effects=True),
-    )(rows).reshape(count * rows.shape[0], rows.shape[1])
-
-
-def scatter_kernel(in_ref, out_ref, held, total, arrived, send_y, recv_y, send_z, recv_z):
+    )(rows.reshape(2, HALF, -1)).reshape(-1, rows.shape[1])
+
+
+SPANS = ((6, 6), (2, 4), (12, 4), (0, 2))
+
+
+def scatter_body(
+    in_ref, out_ref, held, total, arrived, crossed, chain, first,
+    send_y, recv_y, send_z, recv_z, send_t, recv_t, send_u, recv_u,
+):
     me = lax.axis_index("samp")
     z, y = me // NY, lax.rem(me, NY)
-    order = (2, 1, 3, 0)
-
-    def z_copy(way, k, j, own=False):
-        step = 1 - 2 * way
-        far = (UP, DOWN)[way] - k
-        src = in_ref.at[at_place(z + step * far, y + j)] if own else held.at[way, k - 1, j]
-        return remote(
-            src, held.at[way, k, j], send_z.at[way, k, j], recv_z.at[way, k, j],
-            samp=at_place(z + step, y),
-        )
-
-    def z_arrival(way, k, j):
-        step = 1 - 2 * way
-        slot = held.at[way, k, j]
-        return remote(slot, slot, send_z.at[way, k, j], recv_z.at[way, k, j], samp=at_place(z + step, y))
-
-    def add_own(way, k, j):
-        step = 1 - 2 * way
-        far = (UP, DOWN)[way] - k
-        z_arrival(way, k - 1, j).wait_recv()
-        held[way, k - 1, j] = held[way, k - 1, j] + in_ref[at_place(z + step * far, y + j)]
-        z_copy(way, k, j).start()
+    side = NY * NZ
+    steps = [(way, k) for k in range(UP) for way in (0, 1) if k < (UP, DOWN)[way]]
+
+    def target(way, k):
+        return (UP - k) if way == 0 else (NZ - DOWN + k)
+
+    def z_copy(way, k):
+        src = in_ref.at[pl.ds(NY * target(way, k), NY)] if k == 0 else held.at[way, k - 1]
+        return remote(
+            src, held.at[way, k], send_z.at[way, k], recv_z.at[way, k],
+            samp=at_place(z + 1 - 2 * way, y),
+        )
+
+    def u_copy(span, d):
+        start, size = SPANS[span]
+        return remote(
+            in_ref.at[pl.ds(side + d * NZ + start, size)], crossed.at[d, pl.ds(start, size)],
+            send_u.at[span, d], recv_u.at[span, d], samp=at_place(z, y + d),
+        )
+
+    def t_copy(way, k):
+        return remote(
+            first.at[way] if k == 0 else chain.at[way, k - 1], chain.at[way, k],
+            send_t.at[way, k], recv_t.at[way, k], samp=at_place(z + 1 - 2 * way, y),
+        )
 
     def y_copy(d):
         return remote(total.at[d], arrived.at[d], send_y.at[d], recv_y.at[d], samp=at_place(z, y + d))
 
-    pl.semaphore_wait(pltpu.get_barrier_semaphore(), greet("samp", near_peers(z, y)))
-    for j in order:
-        for way in (0, 1):
-            z_copy(way, 0, j, True).start()
-
-    def hop(k, carry):
-        for j in order:
+    ready = set()
+
+    def crossed_sum(off):
+        for span, (start, size) in enumerate(SPANS):
+            if start <= off < start + size and span not in ready:
+                ready.add(span)
+                for d in (1, 3, 2):
+                    u_copy(span, d).wait_recv()
+        return in_ref[side + off] + crossed[1, off] + crossed[2, off] + crossed[3, off]
+
+    for span in range(len(SPANS)):
+        for d in (2, 1, 3):
+            u_copy(span, d).start()
+        if span == 0:
             for way in (0, 1):
-                add_own(way, k, j)
-        return carry
-
-    lax.fori_loop(1, DOWN, hop, 0)
-    for j in order:
-        add_own(0, UP - 1, j)
-    for j in order:
-        z_arrival(1, DOWN - 1, j).wait_recv()
-        z_arrival(0, UP - 1, j).wait_recv()
-        total[j] = held[0, UP - 1, j] + held[1, DOWN - 1, j] + in_ref[at_place(z, y + j)]
-        if j:
-            y_copy(j).start()
-
-    def drain(k, carry):
-        for j in order:
-            for way in (0, 1):
-                z_copy(way, k, j).wait_send()
-        return carry
-
-    for j in order:
-        for way in (0, 1):
-            z_copy(way, 0, j, True).wait_send()
-    lax.fori_loop(1, DOWN, drain, 0)
-    for j in order:
-        z_copy(0, UP - 1, j).wait_send()
+                z_copy(way, 0).start()
+    for way in (0, 1):
+        first[way] = crossed_sum(target(way, 0))
+        t_copy(way, 0).start()
+    for way, k in steps:
+        if (way, k + 1) in steps:
+            z_copy(way, k).wait_recv()
+            held[way, k] = held[way, k] + in_ref[pl.ds(NY * target(way, k + 1), NY)]
+            z_copy(way, k + 1).start()
+            mine = crossed_sum(target(way, k + 1))
+            t_copy(way, k).wait_recv()
+            chain[way, k] = chain[way, k] + mine
+            t_copy(way, k + 1).start()
+    z_copy(1, DOWN - 1).wait_recv()
+    z_copy(0, UP - 1).wait_recv()
+    total[...] = held[0, UP - 1] + held[1, DOWN - 1] + in_ref[pl.ds(0, NY)]
+    for d in (2, 1, 3):
+        y_copy(d).start()
+    mine = crossed_sum(0)
+    t_copy(1, DOWN - 1).wait_recv()
+    t_copy(0, UP - 1).wait_recv()
+    out_ref[pl.ds(HALF, HALF)] = mine + chain[0, UP - 1] + chain[1, DOWN - 1]
+    for way, k in steps:
+        t_copy(way, k).wait_send()
+        z_copy(way, k).wait_send()
+    for span in range(len(SPANS)):
+        for d in (2, 1, 3):
+            u_copy(span, d).wait_send()
     for d in (1, 3, 2):
         y_copy(d).wait()
-    out_ref[...] = total[0] + arrived[1] + arrived[2] + arrived[3]
+    out_ref[pl.ds(0, HALF)] = total[0] + arrived[1] + arrived[2] + arrived[3]
+
+
+def scatter_kernel(in_ref, out_ref, *scratch):
+    me = lax.axis_index("samp")
+    z, y = me // NY, lax.rem(me, NY)
+    pl.semaphore_wait(pltpu.get_barrier_semaphore(), greet("samp", near_peers(z, y)))
+    scatter_body(in_ref, out_ref, *scratch)
 
 
 def owned_of(sums, number):
@@ -202,14 +239,18 @@
     dma = pltpu.SemaphoreType.DMA
     return pl.pallas_call(
         scatter_kernel,
-        out_shape=jax.ShapeDtypeStruct(block, jnp.float32),
+        out_shape=jax.ShapeDtypeStruct((2 * block[0], block[1]), jnp.float32),
         in_specs=vmem(1),
         out_specs=vmem(1)[0],
         scratch_shapes=[
             pltpu.VMEM((2, UP, NY, *block), jnp.float32),
             pltpu.VMEM((NY, *block), jnp.float32),
             pltpu.VMEM((NY, *block), jnp.float32),
-            dma((NY,)), dma((NY,)), dma((2, UP, NY)), dma((2, UP, NY)),
+            pltpu.VMEM((NY, NZ, *block), jnp.float32),
+            pltpu.VMEM((2, UP, *block), jnp.float32),
+            pltpu.VMEM((2, *block), jnp.float32),
+            dma((NY,)), dma((NY,)), dma((2, UP)), dma((2, UP)),
+            dma((2, UP)), dma((2, UP)), dma((len(SPANS), NY)), dma((len(SPANS), NY)),
         ],
         compiler_params=pltpu.CompilerParams(collective_id=number, has_side_effects=True),
     )(sums)
@@ -306,8 +347,16 @@
     space_count = float(per_owner * owners * row_width * hour_count)
     sample_count = float(use_count * samp_dev * owners)
     my_counties = lax.dynamic_index_in_dim(slot_county, owner_index, 0, keepdims=False)
-    county = jnp.take(my_counties, slot_of_sample)
-    place = county // per_owner * PAD + county % per_owner
+    slots = jnp.arange(slot_county.shape[1], dtype=jnp.int32)
+    county = jnp.sum(
+        jnp.where(slots[:, None] == slot_of_sample[None, :], my_counties[:, None], 0), axis=0
+    )
+    owner, row = county // per_owner, county % per_owner
+    far = (owner // NY - owner_index // NY) % NZ
+    beside = (owner % NY - owner_index % NY) % NY
+    upper = (far * NY + beside) * HALF + row
+    lower = ((NY + beside) * NZ + far) * HALF + row - HALF
+    place = jnp.where(row < HALF, upper, lower)
     places = jnp.arange(owners * PAD, dtype=jnp.int32)
     onehot = (places[:, None] == place[None, :]).astype(jnp.bfloat16)
     wide = profiles.astype(jnp.float32)
@@ -339,10 +388,11 @@
     sums = lax.dot_general(
         onehot, two_pieces(weighted, 0), (((1,), (1,)), ((), ())), preferred_element_type=jnp.float32
     )
-    sums = (sums[:, :row_width] + sums[:, row_width:]).reshape(owners, PAD, row_width)
+    sums = (sums[:, :row_width] + sums[:, row_width:]).reshape(2 * owners, HALF, row_width)
     mine = jnp.sum(image * image)
-    row = jnp.arange(PAD, dtype=jnp.int32)[None, :, None]
-    sums = jnp.where(row == per_owner, mine, sums)
+    side = jnp.arange(2 * owners, dtype=jnp.int32)[:, None, None]
+    line = jnp.arange(HALF, dtype=jnp.int32)[None, :, None]
+    sums = jnp.where((side >= owners) & (line == per_owner - HALF), mine, sums)
     owned = owned_of(sums, 5)
     alpha_one = jnp.sqrt(owned[per_owner, 0] / sample_count + epsilon)
     mismatch = owned[:per_owner] / alpha_one - (alpha_one / beta_one) * gap_rows

time: 206 us -> 209 us (1.015)
  Pallas kernels: 153 us -> 161 us
  local copies, waits for them, and re-layouts: 20.2 us -> 12.4 us
    gather x1 -> x0, local copies, waits for them, and re-layouts: 8.58 us -> none  [local(): county = jnp.take(my_counties, slot_of_sample)]
    pallas_call x3, Pallas kernels: 97.4 us -> 105 us  [the longest x2 72.9 us: everyone_of(): pl.pallas_call(gather_kernel, out_shape=jax.ShapeDtypeStruct(whole, jnp.f...]
where the time goes in v4:
time: 209 us; the launch traced here: 207 us
  Pallas kernels  161 us (77%)
  matrix products  15 us (7%)
  other arithmetic  14.7 us (7%)
  local copies, waits for them, and re-layouts  12.4 us (6%)
  between operations  3.91 us (2%)
    pallas_call x2, Pallas kernels, everyone_of(): pl.pallas_call(gather_kernel, out_shape=jax.ShapeDtypeStruct(whole, jnp.f...  72.9 us
    pallas_call x2, Pallas kernels, hour_total(): pl.pallas_call(lambda *refs: hour_kernel(n, *refs), out_shape=jax.ShapeDt...  40.6 us
    pallas_call x1, Pallas kernels, owned_of(): pl.pallas_call(scatter_kernel, out_shape=jax.ShapeDtypeStruct((2 * block[...  32.2 us
    pallas_call x1, Pallas kernels, samp_total(): pl.pallas_call(samp_kernel, out_shape=jax.ShapeDtypeStruct(x.shape, jnp.f...  15.7 us
    dot_general x2, matrix products, backward(): lax.dot_general(pieces, onehot, (((0,), (0,)), ((), ())), preferred_eleme...  9.88 us
    reduce_sum x2, other arithmetic, backward(): square = jnp.sum(everyone * everyone)  5.13 us
    dot_general x1, matrix products, local(): lax.dot_general(onehot, two_pieces(weighted, 0), (((1,), (1,)), ((), ()))...  5.08 us

profile of v4, /device:TPU:1, one launch (start us, length us, event | category | flops | bytes accessed | tf_op | source)
XLA Modules:
  0.0 207.5 jit_solution(4913676328718469264)
XLA Ops:
  0.7 0.9 copy-done
  1.6 1.8 select_reduce_fusion
  3.5 0.9 copy.13
  5.1 42.1 %shard_map.67 = f32[128,24,128]{2,1,0:T(8,128)} custom-call(f32[2,24,128]{2,1,0:T(8,128)} %bitcast.25), custom_call_target="tpu_custom_call" | custom-call | tf_op jit(solution)/shard_map/pallas_call | solution.py:130
  47.2 2.5 %multiply_reduce_fusion.1 = f32[]{:T(128)} fusion(f32[128,24,128]{2,1,0:T(8,128)} %shard_map.67), kind=kLoop, calls=%fused_computation.23 | loop fusion | flops 786431 | bytes 1572868 | tf_op jit(solution)/shard_map/reduce_sum | solution.py:369
  50.0 4.9 %fusion.2 = f32[256,2048]{1,0:T(8,128)S(1)} fusion(s32[2048]{0:T(1024)S(1)} %add_select_fusion.6, bf16[3072,128]{1,0:T(8,128)(2,1)S(1)} %get-tuple-element.19, bf16[3072,128]{1,0:T(8,128)(2,1)S(1)} %get-tuple-element.18), kind=kOutput, calls=%fused_computation.3 | convolution fusion | flops 3230662656 | bytes 3678208 | tf_op jit(solution)/shard_map/dot_general | solution.py:371
  55.2 1.3 concatenate.19.refs_0_
  56.5 17.6 %shard_map.68 = f32[72,128]{1,0:T(8,128)} custom-call(f32[72,128]{1,0:T(8,128)} %concatenate.19.refs_0_), custom_call_target="tpu_custom_call" | custom-call | tf_op jit(solution)/shard_map/pallas_call | solution.py:279
  74.1 1.2 slice.42
  75.9 1.4 multiply_reduce_fusion.3
  77.6 5.1 %fusion.1 = f32[3072,256]{1,0:T(8,128)S(1)} fusion(s32[2048]{0:T(1024)S(1)} %add_select_fusion.6, bf16[128,2048]{1,0:T(8,128)(2,1)S(1)} %get-tuple-element.21, bf16[128,2048]{1,0:T(8,128)(2,1)S(1)} %get-tuple-element.20), kind=kOutput, calls=%fused_computation.2 | convolution fusion | flops 3229614080 | bytes 4202496 | tf_op jit(solution)/shard_map/dot_general | solution.py:388
  82.8 2.1 %broadcast_select_fusion.in_ref = f32[128,24,128]{2,1,0:T(8,128)} fusion(f32[128,24,128]{2,1,0:T(8,128)S(1)} %bitcast.23, f32[]{:T(128)} %get-tuple-element.14, pred[128,24]{1,0:T(8,128)(4,1)S(1)} %broadcast_and_fusion), kind=kLoop, calls=%fused_computation.37 | loop fusion | flops 393216 | bytes 3148804 | tf_op jit(solution)/shard_map/jit(_where)/select_n | solution.py:395
  85.0 32.2 %shard_map.69 = f32[48,128]{1,0:T(8,128)} custom-call(f32[128,24,128]{2,1,0:T(8,128)} %broadcast_select_fusion.in_ref), custom_call_target="tpu_custom_call" | custom-call | tf_op jit(solution)/shard_map/pallas_call | solution.py:240
  117.2 1.2 slice.45
  120.5 30.8 %shard_map.70 = f32[128,24,128]{2,1,0:T(8,128)} custom-call(f32[2,24,128]{2,1,0:T(8,128)} %bitcast.24), custom_call_target="tpu_custom_call" | custom-call | tf_op jit(solution)/shard_map/pallas_call | solution.py:130
  151.3 2.6 %multiply_reduce_fusion = f32[]{:T(128)} fusion(f32[128,24,128]{2,1,0:T(8,128)} %shard_map.70), kind=kLoop, calls=%fused_computation.22 | loop fusion | flops 786431 | bytes 1572868 | tf_op jit(solution)/shard_map/reduce_sum | solution.py:369
  154.2 4.9 %fusion = f32[256,2048]{1,0:T(8,128)S(1)} fusion(s32[2048]{0:T(1024)S(1)} %add_select_fusion.6, bf16[3072,128]{1,0:T(8,128)(2,1)S(1)} %get-tuple-element.17, bf16[3072,128]{1,0:T(8,128)(2,1)S(1)} %get-tuple-element.16), kind=kOutput, calls=%fused_computation.1 | convolution fusion | flops 3230662656 | bytes 3678208 | tf_op jit(solution)/shard_map/dot_general | solution.py:371
  159.4 1.2 concatenate.22.refs_0_
  160.7 23.0 %shard_map.71 = f32[72,128]{1,0:T(8,128)} custom-call(f32[72,128]{1,0:T(8,128)} %concatenate.22.refs_0_), custom_call_target="tpu_custom_call" | custom-call | tf_op jit(solution)/shard_map/pallas_call | solution.py:279
  183.8 1.2 slice.49
  185.8 1.4 multiply_reduce_fusion.2
  187.2 1.2 broadcast_in_dim.44.in_ref
  188.5 15.7 %shard_map.72 = f32[8,128]{1,0:T(8,128)} custom-call(f32[8,128]{1,0:T(8,128)} %broadcast_in_dim.44.in_ref), custom_call_target="tpu_custom_call" | custom-call | tf_op jit(solution)/shard_map/pallas_call | solution.py:318
  204.2 1.2 slice.51
  (32 shorter events, 5.1 us)
Async XLA Ops:
  0.6 1.0 copy-start
  47.1 2.5 %copy-start.1 = (f32[128,24,128]{2,1,0:T(8,128)S(1)}, f32[128,24,128]{2,1,0:T(8,128)}, u32[]{:S(2)}) copy-start(f32[128,24,128]{2,1,0:T(8,128)} %shard_map.67) | copy-start | bytes 4718596
  49.9 4.9 %copy-start.3 = (bf16[4,32,2048]{2,1,0:T(8,128)(2,1)S(1)}, bf16[4,32,2048]{2,1,0:T(8,128)(2,1)}, u32[]{:S(2)}) copy-start(bf16[4,32,2048]{2,1,0:T(8,128)(2,1)} %param.5) | copy-start | bytes 1572868
  151.3 2.6 %copy-start.2 = (f32[128,24,128]{2,1,0:T(8,128)S(1)}, f32[128,24,128]{2,1,0:T(8,128)}, u32[]{:S(2)}) copy-start(f32[128,24,128]{2,1,0:T(8,128)} %shard_map.70) | copy-start | bytes 4718596
  159.1 26.7 %copy-start.4 = (f32[72,128]{1,0:T(8,128)S(1)}, f32[72,128]{1,0:T(8,128)}, u32[]{:S(2)}) copy-start(f32[72,128]{1,0:T(8,128)} %shard_map.68) | copy-start | bytes 110596

commit v5 on v2

--- a/solution.py
+++ b/solution.py
@@ -130,7 +130,7 @@
     )(rows).reshape(count * rows.shape[0], rows.shape[1])
 
 
-def scatter_kernel(in_ref, out_ref, held, total, arrived, send_y, recv_y, send_z, recv_z):
+def scatter_body(in_ref, out_ref, held, total, arrived, send_y, recv_y, send_z, recv_z):
     me = lax.axis_index("samp")
     z, y = me // NY, lax.rem(me, NY)
     order = (2, 1, 3, 0)
@@ -159,7 +159,6 @@
     def y_copy(d):
         return remote(total.at[d], arrived.at[d], send_y.at[d], recv_y.at[d], samp=at_place(z, y + d))
 
-    pl.semaphore_wait(pltpu.get_barrier_semaphore(), greet("samp", near_peers(z, y)))
     for j in order:
         for way in (0, 1):
             z_copy(way, 0, j, True).start()
@@ -197,22 +196,46 @@
     out_ref[...] = total[0] + arrived[1] + arrived[2] + arrived[3]
 
 
-def owned_of(sums, number):
+def middle_kernel(sample_count, real, in_ref, gap_ref, beta_ref, all_ref, mine_ref, owned, fresh, got, *rest):
+    me = lax.axis_index("samp")
+    z, y = me // NY, lax.rem(me, NY)
+    pl.semaphore_wait(pltpu.get_barrier_semaphore(), greet("samp", near_peers(z, y)))
+    scatter_body(in_ref, owned, *rest[:7])
+    alpha_one = jnp.sqrt(owned[pl.ds(real, 1)] / sample_count + epsilon)
+    beta_one = beta_ref[pl.ds(0, 1)]
+    mismatch = owned[...] / alpha_one - (alpha_one / beta_one) * gap_ref[...]
+    row = lax.broadcasted_iota(jnp.int32, mismatch.shape, 0)
+    mismatch = jnp.where(row < real, mismatch, 0.0)
+    fresh[...] = mismatch
+    mine_ref[pl.ds(0, PAD)] = mismatch
+    mine_ref[pl.ds(PAD, 8)] = jnp.broadcast_to(alpha_one, (8, 128))
+    gather_body(fresh, got, *rest[7:])
+    all_ref[...] = got[...]
+
+
+def middle(sums, gap, beta, sample_count, real, number):
     block = sums.shape[1:]
     dma = pltpu.SemaphoreType.DMA
+    sems = [dma((NY,)), dma((NY,)), dma((2, UP, NY)), dma((2, UP, NY))]
     return pl.pallas_call(
-        scatter_kernel,
-        out_shape=jax.ShapeDtypeStruct(block, jnp.float32),
-        in_specs=vmem(1),
-        out_specs=vmem(1)[0],
+        lambda *refs: middle_kernel(sample_count, real, *refs),
+        out_shape=[
+            jax.ShapeDtypeStruct(sums.shape, jnp.float32),
+            jax.ShapeDtypeStruct((PAD + 8, block[1]), jnp.float32),
+        ],
+        in_specs=vmem(3),
+        out_specs=vmem(2),
         scratch_shapes=[
+            pltpu.VMEM(block, jnp.float32),
+            pltpu.VMEM(block, jnp.float32),
+            pltpu.VMEM(sums.shape, jnp.float32),
             pltpu.VMEM((2, UP, NY, *block), jnp.float32),
             pltpu.VMEM((NY, *block), jnp.float32),
             pltpu.VMEM((NY, *block), jnp.float32),
-            dma((NY,)), dma((NY,)), dma((2, UP, NY)), dma((2, UP, NY)),
+            *sems, *sems,
         ],
         compiler_params=pltpu.CompilerParams(collective_id=number, has_side_effects=True),
-    )(sums)
+    )(sums, gap, beta)
 
 
 def hour_kernel(n, in_ref, out_ref, arrived, send_sem, recv_sem):
@@ -245,22 +268,43 @@
     )(x)
 
 
-def samp_kernel(in_ref, out_ref, first, middle, second, send_y, recv_y, send_z, recv_z):
-    me = lax.axis_index("samp")
+def last_kernel(
+    n, space_count, in_ref, vector_ref, out_ref, arrived, first, middle, second, start,
+    send_h, recv_h, send_y, recv_y, send_z, recv_z,
+):
+    me, hour = lax.axis_index("samp"), lax.axis_index("hour")
     z, y = me // NY, lax.rem(me, NY)
+    order = [n // 2] + [d for d in range(1, n) if d != n // 2]
     far_first = sorted(range(1, NZ), key=lambda d: -min(d, NZ - d))
+    rows = vector_ref.shape[0]
+
+    def h_copy(d):
+        return remote(in_ref, arrived.at[d], send_h.at[d], recv_h.at[d], hour=lax.rem(hour + d, n))
 
     def y_copy(d):
-        return remote(in_ref, first.at[d], send_y.at[d], recv_y.at[d], samp=at_place(z, y + d))
+        return remote(start, first.at[d], send_y.at[d], recv_y.at[d], samp=at_place(z, y + d))
 
     def z_copy(d):
         return remote(middle, second.at[d], send_z.at[d], recv_z.at[d], samp=at_place(z + d, y))
 
     peers = [at_place(z + d, y) for d in far_first] + [at_place(z, y + d) for d in (2, 1, 3)]
-    pl.semaphore_wait(pltpu.get_barrier_semaphore(), greet("samp", peers))
+    count = greet("samp", peers) + greet("hour", [lax.rem(hour + d, n) for d in order])
+    pl.semaphore_wait(pltpu.get_barrier_semaphore(), count)
+    for d in order:
+        h_copy(d).start()
+    arrived[0] = in_ref[...]
+    for d in order:
+        h_copy(d).wait()
+    total = jnp.sum(arrived[...], axis=0)
+    square = total[rows:]
+    beta_two = jnp.sqrt(square[:1] / space_count + epsilon)
+    image_two = total[:rows] / beta_two - beta_two * vector_ref[...]
+    out_ref[pl.ds(0, rows)] = image_two
+    out_ref[pl.ds(rows, 8)] = square
+    start[...] = jnp.full(start.shape, jnp.sum(image_two * image_two))
     for d in (2, 1, 3):
         y_copy(d).start()
-    first[0] = in_ref[...]
+    first[0] = start[...]
     for d in (1, 3, 2):
         y_copy(d).wait()
     middle[...] = jnp.sum(first[...], axis=0)
@@ -269,24 +313,28 @@
     second[0] = middle[...]
     for d in far_first[::-1]:
         z_copy(d).wait()
-    out_ref[...] = jnp.sum(second[...], axis=0)
-
-
-def samp_total(x, number):
+    out_ref[pl.ds(rows + 8, 8)] = jnp.sum(second[...], axis=0)
+
+
+def last_sums(x, vector, space_count, number):
+    n = lax.axis_size("hour")
     dma = pltpu.SemaphoreType.DMA
+    small = (8, 128)
     return pl.pallas_call(
-        samp_kernel,
-        out_shape=jax.ShapeDtypeStruct(x.shape, jnp.float32),
-        in_specs=vmem(1),
+        lambda *refs: last_kernel(n, space_count, *refs),
+        out_shape=jax.ShapeDtypeStruct((x.shape[0] + 8, 128), jnp.float32),
+        in_specs=vmem(2),
         out_specs=vmem(1)[0],
         scratch_shapes=[
-            pltpu.VMEM((NY, *x.shape), jnp.float32),
-            pltpu.VMEM(x.shape, jnp.float32),
-            pltpu.VMEM((NZ, *x.shape), jnp.float32),
-            dma((NY,)), dma((NY,)), dma((NZ,)), dma((NZ,)),
+            pltpu.VMEM((n, *x.shape), jnp.float32),
+            pltpu.VMEM((NY, *small), jnp.float32),
+            pltpu.VMEM(small, jnp.float32),
+            pltpu.VMEM((NZ, *small), jnp.float32),
+            pltpu.VMEM(small, jnp.float32),
+            dma((n,)), dma((n,)), dma((NY,)), dma((NY,)), dma((NZ,)), dma((NZ,)),
         ],
         compiler_params=pltpu.CompilerParams(collective_id=number, has_side_effects=True),
-    )(x)
+    )(x, vector)
 
 
 def two_pieces(x, axis):
@@ -306,7 +354,10 @@
     space_count = float(per_owner * owners * row_width * hour_count)
     sample_count = float(use_count * samp_dev * owners)
     my_counties = lax.dynamic_index_in_dim(slot_county, owner_index, 0, keepdims=False)
-    county = jnp.take(my_counties, slot_of_sample)
+    slots = jnp.arange(slot_county.shape[1], dtype=jnp.int32)
+    county = jnp.sum(
+        jnp.where(slots[:, None] == slot_of_sample[None, :], my_counties[:, None], 0), axis=0
+    )
     place = county // per_owner * PAD + county % per_owner
     places = jnp.arange(owners * PAD, dtype=jnp.int32)
     onehot = (places[:, None] == place[None, :]).astype(jnp.bfloat16)
@@ -315,8 +366,8 @@
     def padded(rows):
         return jnp.pad(rows, ((0, PAD - per_owner), (0, 0)))
 
-    def backward(rows, number):
-        everyone = everyone_of(padded(rows), number)
+    def backward(everyone):
+        everyone = everyone.reshape(-1, row_width)
         square = jnp.sum(everyone * everyone)
         pieces = two_pieces(everyone, 1)
         spread = lax.dot_general(
@@ -324,15 +375,14 @@
         )
         spread = (spread[:row_width] + spread[row_width:]).reshape(use_count, hour_dev, samp_dev)
         partial = jnp.sum(wide * spread, axis=1)
-        rest = jnp.full((8, 128), square)
-        total = hour_total(jnp.concatenate([partial.reshape(-1, 128), rest], axis=0), number + 1)
-        return total[:-8].reshape(use_count, samp_dev), total[-1, 0]
+        return jnp.concatenate([partial.reshape(-1, 128), jnp.full((8, 128), square)], axis=0)
 
     def my_share(x):
         return lax.dynamic_slice_in_dim(x, hour_index * share_len, share_len, 1)
 
     gap_rows = load_gap.reshape(per_owner, row_width)
-    plain, gap_total = backward(gap_rows, 1)
+    total = hour_total(backward(everyone_of(padded(gap_rows), 1)), 2)
+    plain, gap_total = total[:-8].reshape(use_count, samp_dev), total[-1, 0]
     beta_one = jnp.sqrt(gap_total / space_count + epsilon)
     image = plain / beta_one
     weighted = (wide * image[:, None, :]).reshape(row_width, samp_dev)
@@ -343,16 +393,16 @@
     mine = jnp.sum(image * image)
     row = jnp.arange(PAD, dtype=jnp.int32)[None, :, None]
     sums = jnp.where(row == per_owner, mine, sums)
-    owned = owned_of(sums, 5)
-    alpha_one = jnp.sqrt(owned[per_owner, 0] / sample_count + epsilon)
-    mismatch = owned[:per_owner] / alpha_one - (alpha_one / beta_one) * gap_rows
-    back, mismatch_total = backward(mismatch, 3)
-    beta_two = jnp.sqrt(mismatch_total / space_count + epsilon)
+    everyone, owned = middle(
+        sums, padded(gap_rows), jnp.full((8, 128), beta_one), sample_count, per_owner, 3
+    )
+    mismatch, alpha_one = owned[:per_owner], owned[PAD, 0]
+    vector_one = image / alpha_one
+    last = last_sums(backward(everyone), vector_one.reshape(-1, 128), space_count, 4)
+    beta_two = jnp.sqrt(last[-16, 0] / space_count + epsilon)
+    alpha_two = jnp.sqrt(last[-1, 0] / sample_count + epsilon)
+    image_two = last[:-16].reshape(use_count, samp_dev)
     load_dir = mismatch / beta_two
-    vector_one = image / alpha_one
-    image_two = back / beta_two - beta_two * vector_one
-    second_total = samp_total(jnp.full((8, 128), jnp.sum(image_two * image_two)), 6)[0, 0]
-    alpha_two = jnp.sqrt(second_total / sample_count + epsilon)
     rho_value = jnp.sqrt(alpha_one * alpha_one + beta_two * beta_two)
     cosine = alpha_one / rho_value
     sine = beta_two / rho_value

time: 206 us -> 189 us (0.917)
  local copies, waits for them, and re-layouts: 20.2 us -> 10.8 us
  Pallas kernels: 153 us -> 145 us
    pallas_call x2, Pallas kernels: 45.6 us -> 88.1 us  [the longest x1 54.8 us: middle(): pl.pallas_call(lambda *refs: middle_kernel(sample_count, real, *refs), ou...]
    pallas_call x2 -> x1, Pallas kernels: 67.7 us -> 40.1 us  [everyone_of(): pl.pallas_call(gather_kernel, out_shape=jax.ShapeDtypeStruct((count, *row...]
    pallas_call x2 -> x1, Pallas kernels: 39.2 us -> 16.4 us  [hour_total(): pl.pallas_call(lambda *refs: hour_kernel(n, *refs), out_shape=jax.ShapeDt...]
    gather x1 -> x0, local copies, waits for them, and re-layouts: 8.58 us -> none  [local(): county = jnp.take(my_counties, slot_of_sample)]
where the time goes in v5:
time: 189 us; the launch traced here: 188 us
  Pallas kernels  145 us (77%)
  matrix products  14.8 us (8%)
  other arithmetic  12.3 us (7%)
  local copies, waits for them, and re-layouts  10.8 us (6%)
  between operations  5.67 us (3%)
    pallas_call x1, Pallas kernels, middle(): pl.pallas_call(lambda *refs: middle_kernel(sample_count, real, *refs), ou...  54.8 us
    pallas_call x1, Pallas kernels, everyone_of(): pl.pallas_call(gather_kernel, out_shape=jax.ShapeDtypeStruct((count, *row...  40.1 us
    pallas_call x1, Pallas kernels, last_sums(): pl.pallas_call(lambda *refs: last_kernel(n, space_count, *refs), out_shap...  33.3 us
    pallas_call x1, Pallas kernels, hour_total(): pl.pallas_call(lambda *refs: hour_kernel(n, *refs), out_shape=jax.ShapeDt...  16.4 us
    dot_general x2, matrix products, backward(): lax.dot_general(pieces, onehot, (((0,), (0,)), ((), ())), preferred_eleme...  9.88 us
    reduce_sum x2, other arithmetic, backward(): square = jnp.sum(everyone * everyone)  5.07 us
    dot_general x1, matrix products, local(): lax.dot_general(onehot, two_pieces(weighted, 0), (((1,), (1,)), ((), ()))...  4.9 us

profile of v5, /device:TPU:1, one launch (start us, length us, event | category | flops | bytes accessed | tf_op | source)
XLA Modules:
  0.0 188.3 jit_solution(10847926009485793311)
XLA Ops:
  0.7 0.9 copy-done
  1.6 1.8 select_reduce_fusion
  3.4 0.9 copy.13
  4.3 0.6 pad.7.in_ref.refs_1_
  5.0 40.1 %shard_map.67 = f32[64,48,128]{2,1,0:T(8,128)} custom-call(f32[48,128]{1,0:T(8,128)} %pad.7.in_ref.refs_1_), custom_call_target="tpu_custom_call" | custom-call | tf_op jit(solution)/shard_map/pallas_call | solution.py:120
  45.1 2.5 %multiply_reduce_fusion.1 = f32[]{:T(128)} fusion(f32[64,48,128]{2,1,0:T(8,128)} %shard_map.67), kind=kLoop, calls=%fused_computation.23 | loop fusion | flops 786431 | bytes 1572868 | tf_op jit(solution)/shard_map/reduce_sum | solution.py:371
  47.9 4.9 %fusion.2 = f32[256,2048]{1,0:T(8,128)S(1)} fusion(s32[2048]{0:T(1024)S(1)} %fusion.21, bf16[3072,128]{1,0:T(8,128)(2,1)S(1)} %get-tuple-element.21, bf16[3072,128]{1,0:T(8,128)(2,1)S(1)} %get-tuple-element.20), kind=kOutput, calls=%fused_computation.3 | convolution fusion | flops 3230662656 | bytes 3678208 | tf_op jit(solution)/shard_map/dot_general | solution.py:373
  53.2 1.3 concatenate.19.refs_0_
  54.4 16.4 %shard_map.68 = f32[72,128]{1,0:T(8,128)} custom-call(f32[72,128]{1,0:T(8,128)} %concatenate.19.refs_0_), custom_call_target="tpu_custom_call" | custom-call | tf_op jit(solution)/shard_map/pallas_call | solution.py:261
  70.9 1.2 slice.42
  72.8 0.6 broadcast_in_dim.43.refs_2_
  73.4 1.4 multiply_reduce_fusion.2
  75.0 4.9 %fusion.1 = f32[3072,256]{1,0:T(8,128)S(1)} fusion(s32[2048]{0:T(1024)S(1)} %fusion.21, bf16[128,2048]{1,0:T(8,128)(2,1)S(1)} %get-tuple-element.23, bf16[128,2048]{1,0:T(8,128)(2,1)S(1)} %get-tuple-element.22), kind=kOutput, calls=%fused_computation.2 | convolution fusion | flops 3229614080 | bytes 4202496 | tf_op jit(solution)/shard_map/dot_general | solution.py:389
  80.1 2.0 %broadcast_select_fusion.refs_0_ = f32[64,48,128]{2,1,0:T(8,128)} fusion(f32[64,48,128]{2,1,0:T(8,128)S(1)} %bitcast.21, f32[]{:T(128)} %get-tuple-element.16, pred[48]{0:T(512)(128)(4,1)S(1)} %iota_compare_fusion.5), kind=kLoop, calls=%fused_computation.37 | loop fusion | flops 393216 | bytes 3145780 | tf_op jit(solution)/shard_map/jit(_where)/select_n | solution.py:395
  82.1 54.8 %shard_map.69 = (f32[64,48,128]{2,1,0:T(8,128)}, f32[56,128]{1,0:T(8,128)}) custom-call(f32[64,48,128]{2,1,0:T(8,128)} %broadcast_select_fusion.refs_0_, f32[48,128]{1,0:T(8,128)} %pad.7.in_ref.refs_1_, f32[8,128]{1,0:T(8,128)} %broadcast_in_dim.43.refs_2_), custom_call_target="tpu_custom_call" | custom-call | tf_op jit(solution)/shard_map/pallas_call | solution.py:220
  136.9 2.5 %multiply_reduce_fusion = f32[]{:T(128)} fusion(f32[64,48,128]{2,1,0:T(8,128)} %get-tuple-element.6), kind=kLoop, calls=%fused_computation.22 | loop fusion | flops 786431 | bytes 1572868 | tf_op jit(solution)/shard_map/reduce_sum | solution.py:371
  139.5 1.2 slice.45
  142.9 4.9 %fusion = f32[256,2048]{1,0:T(8,128)S(1)} fusion(s32[2048]{0:T(1024)S(1)} %fusion.21, bf16[3072,128]{1,0:T(8,128)(2,1)S(1)} %get-tuple-element.19, bf16[3072,128]{1,0:T(8,128)(2,1)S(1)} %get-tuple-element.18), kind=kOutput, calls=%fused_computation.1 | convolution fusion | flops 3230662656 | bytes 3678208 | tf_op jit(solution)/shard_map/dot_general | solution.py:373
  148.2 1.3 concatenate.22.refs_0_
  149.4 33.3 %shard_map.70 = f32[80,128]{1,0:T(8,128)} custom-call(f32[72,128]{1,0:T(8,128)} %concatenate.22.refs_0_, f32[64,128]{1,0:T(8,128)} %copy-done.4), custom_call_target="tpu_custom_call" | custom-call | tf_op jit(solution)/shard_map/pallas_call | solution.py:323
  182.7 1.2 fusion.26
  186.1 0.8 slice.49
  186.9 0.6 divide_subtract_fusion
  187.5 0.7 copy.14
  (30 shorter events, 1.6 us)
Async XLA Ops:
  0.6 1.0 copy-start
  45.1 2.5 %copy-start.1 = (f32[64,48,128]{2,1,0:T(8,128)S(1)}, f32[64,48,128]{2,1,0:T(8,128)}, u32[]{:S(2)}) copy-start(f32[64,48,128]{2,1,0:T(8,128)} %shard_map.67) | copy-start | bytes 4718596
  47.9 5.0 %copy-start.3 = (bf16[4,32,2048]{2,1,0:T(8,128)(2,1)S(1)}, bf16[4,32,2048]{2,1,0:T(8,128)(2,1)}, u32[]{:S(2)}) copy-start(bf16[4,32,2048]{2,1,0:T(8,128)(2,1)} %param.5) | copy-start | bytes 1572868
  82.1 60.5 %copy-start.5 = (f32[72,128]{1,0:T(8,128)S(1)}, f32[72,128]{1,0:T(8,128)}, u32[]{:S(2)}) copy-start(f32[72,128]{1,0:T(8,128)} %shard_map.68) | copy-start | bytes 110596
  136.9 5.7 %copy-start.2 = (f32[64,48,128]{2,1,0:T(8,128)S(1)}, f32[64,48,128]{2,1,0:T(8,128)}, u32[]{:S(2)}) copy-start(f32[64,48,128]{2,1,0:T(8,128)} %get-tuple-element.6) | copy-start | bytes 4718596
  142.6 5.2 %copy-start.4 = (f32[64,128]{1,0:T(8,128)}, f32[64,128]{1,0:T(8,128)S(1)}, u32[]{:S(2)}) copy-start(f32[64,128]{1,0:T(8,128)S(1)} %slice_divide_fusion.refs_1_) | copy-start | bytes 98308
  147.8 39.1 %copy-start.6 = (f32[56,128]{1,0:T(8,128)S(1)}, f32[56,128]{1,0:T(8,128)}, u32[]{:S(2)}) copy-start(f32[56,128]{1,0:T(8,128)} %get-tuple-element.5) | copy-start | bytes 86020

commit v6 on v2

--- a/solution.py
+++ b/solution.py
@@ -36,7 +36,7 @@
     return [at_place(z, y + d) for d in range(1, NY)] + [at_place(z + 1, y), at_place(z - 1, y)]
 
 
-def gather_body(in_ref, out_ref, send_y, recv_y, send_z, recv_z):
+def gather_body(use, in_ref, out_ref, send_y, recv_y, send_z, recv_z):
     me = lax.axis_index("samp")
     z, y = me // NY, lax.rem(me, NY)
 
@@ -69,12 +69,15 @@
         y_arrival(j).wait_recv()
         z_copy(0, 0, j).start()
         z_copy(1, 0, j).start()
+    use(z)
 
     def hop(k, carry):
         for j in (0, 1, 3, 2):
             for way in (0, 1):
                 z_arrival(way, k - 1, j).wait_recv()
                 z_copy(way, k, j).start()
+        use(lax.rem(z + NZ - k, NZ))
+        use(lax.rem(z + k, NZ))
         return carry
 
     lax.fori_loop(1, DOWN, hop, 0)
@@ -82,6 +85,8 @@
         z_arrival(0, UP - 2, j).wait_recv()
         z_copy(0, UP - 1, j).start()
         z_arrival(1, DOWN - 1, j).wait_recv()
+    use(lax.rem(z + NZ - DOWN, NZ))
+    use(lax.rem(z + DOWN, NZ))
     for d in (2, 1, 3):
         y_copy(d).wait_send()
     z_copy(0, 0, 0, True).wait_send()
@@ -100,37 +105,107 @@
     for j in (0, 1, 3, 2):
         z_copy(0, UP - 1, j).wait_send()
         z_arrival(0, UP - 1, j).wait_recv()
-
-
-def gather_kernel(in_ref, out_ref, got, send_y, recv_y, send_z, recv_z):
+    use(lax.rem(z + NZ - UP, NZ))
+
+
+def spread_into(acc, square, got, place_ref):
+    bundle = NY * PAD
+    acc[...] = jnp.zeros_like(acc)
+    square[...] = jnp.zeros_like(square)
+
+    def use(z):
+        block = got[pl.ds(z * NY, NY)].reshape(bundle, 128)
+        high = block.astype(jnp.bfloat16)
+        low = (block - high.astype(jnp.float32)).astype(jnp.bfloat16)
+        both = jnp.concatenate([high, low], axis=1)
+        places = lax.broadcasted_iota(jnp.int32, (bundle, place_ref.shape[1]), 0) + z * bundle
+        hit = jnp.where(places == place_ref[...], 1.0, 0.0).astype(jnp.bfloat16)
+        acc[...] += lax.dot_general(
+            both, hit, (((0,), (0,)), ((), ())), preferred_element_type=jnp.float32
+        )
+        square[...] += jnp.sum((block * block).reshape(bundle // 8, 8, 128), axis=0)
+
+    return use
+
+
+def fold(acc, square, prof_ref, part):
+    uses, hours, width = prof_ref.shape
+    for e in range(uses):
+        here = acc[pl.ds(e * hours, hours)] + acc[pl.ds((uses + e) * hours, hours)]
+        line = jnp.sum(here * prof_ref[e].astype(jnp.float32), axis=0, keepdims=True)
+        for c in range(width // 128):
+            part[pl.ds(e * (width // 128) + c, 1)] = line[:, c * 128:(c + 1) * 128]
+    part[pl.ds(uses * width // 128, 8)] = jnp.full((8, 128), jnp.sum(square[...]))
+
+
+def hour_peers(n):
+    return [n // 2] + [d for d in range(1, n) if d != n // 2]
+
+
+def hour_body(n, part, arrived, send_h, recv_h):
+    me = lax.axis_index("hour")
+
+    def copy(d):
+        return remote(part, arrived.at[d], send_h.at[d], recv_h.at[d], hour=lax.rem(me + d, n))
+
+    for d in hour_peers(n):
+        copy(d).start()
+    arrived[0] = part[...]
+    for d in hour_peers(n):
+        copy(d).wait()
+    return jnp.sum(arrived[...], axis=0)
+
+
+def greet_hours(n):
+    hour = lax.axis_index("hour")
+    return greet("hour", [lax.rem(hour + d, n) for d in hour_peers(n)])
+
+
+def first_kernel(n, in_ref, place_ref, prof_ref, out_ref, got, acc, square, part, arrived, *sems):
     me = lax.axis_index("samp")
     z, y = me // NY, lax.rem(me, NY)
-    pl.semaphore_wait(pltpu.get_barrier_semaphore(), greet("samp", near_peers(z, y)))
-    gather_body(in_ref, got, send_y, recv_y, send_z, recv_z)
-    out_ref[...] = got[...]
+    count = greet("samp", near_peers(z, y)) + greet_hours(n)
+    pl.semaphore_wait(pltpu.get_barrier_semaphore(), count)
+    gather_body(spread_into(acc, square, got, place_ref), in_ref, got, *sems[:4])
+    fold(acc, square, prof_ref, part)
+    out_ref[...] = hour_body(n, part, arrived, *sems[4:])
 
 
 def vmem(count):
     return [pl.BlockSpec(memory_space=pltpu.VMEM)] * count
 
 
-def everyone_of(rows, number):
-    count = NY * NZ
+def gather_sems():
+    dma = pltpu.SemaphoreType.DMA
+    return [dma((NY,)), dma((NY,)), dma((2, UP, NY)), dma((2, UP, NY))]
+
+
+def spread_scratch(n, width, uses):
+    part = (uses * width // 128 + 8, 128)
+    return [
+        pltpu.VMEM((NY * NZ, PAD, 128), jnp.float32),
+        pltpu.VMEM((256, width), jnp.float32),
+        pltpu.VMEM((8, 128), jnp.float32),
+        pltpu.VMEM(part, jnp.float32),
+        pltpu.VMEM((n, *part), jnp.float32),
+    ]
+
+
+def first_total(rows, place, profiles, number):
+    n = lax.axis_size("hour")
+    uses, _, width = profiles.shape
     dma = pltpu.SemaphoreType.DMA
     return pl.pallas_call(
-        gather_kernel,
-        out_shape=jax.ShapeDtypeStruct((count, *rows.shape), jnp.float32),
-        in_specs=vmem(1),
+        lambda *refs: first_kernel(n, *refs),
+        out_shape=jax.ShapeDtypeStruct((uses * width // 128 + 8, 128), jnp.float32),
+        in_specs=vmem(3),
         out_specs=vmem(1)[0],
-        scratch_shapes=[
-            pltpu.VMEM((count, *rows.shape), jnp.float32),
-            dma((NY,)), dma((NY,)), dma((2, UP, NY)), dma((2, UP, NY)),
-        ],
+        scratch_shapes=[*spread_scratch(n, width, uses), *gather_sems(), dma((n,)), dma((n,))],
         compiler_params=pltpu.CompilerParams(collective_id=number, has_side_effects=True),
-    )(rows).reshape(count * rows.shape[0], rows.shape[1])
-
-
-def scatter_kernel(in_ref, out_ref, held, total, arrived, send_y, recv_y, send_z, recv_z):
+    )(rows, place, profiles)
+
+
+def scatter_body(in_ref, out_ref, held, total, arrived, send_y, recv_y, send_z, recv_z):
     me = lax.axis_index("samp")
     z, y = me // NY, lax.rem(me, NY)
     order = (2, 1, 3, 0)
@@ -159,7 +234,6 @@
     def y_copy(d):
         return remote(total.at[d], arrived.at[d], send_y.at[d], recv_y.at[d], samp=at_place(z, y + d))
 
-    pl.semaphore_wait(pltpu.get_barrier_semaphore(), greet("samp", near_peers(z, y)))
     for j in order:
         for way in (0, 1):
             z_copy(way, 0, j, True).start()
@@ -197,70 +271,47 @@
     out_ref[...] = total[0] + arrived[1] + arrived[2] + arrived[3]
 
 
-def owned_of(sums, number):
-    block = sums.shape[1:]
-    dma = pltpu.SemaphoreType.DMA
-    return pl.pallas_call(
-        scatter_kernel,
-        out_shape=jax.ShapeDtypeStruct(block, jnp.float32),
-        in_specs=vmem(1),
-        out_specs=vmem(1)[0],
-        scratch_shapes=[
-            pltpu.VMEM((2, UP, NY, *block), jnp.float32),
-            pltpu.VMEM((NY, *block), jnp.float32),
-            pltpu.VMEM((NY, *block), jnp.float32),
-            dma((NY,)), dma((NY,)), dma((2, UP, NY)), dma((2, UP, NY)),
-        ],
-        compiler_params=pltpu.CompilerParams(collective_id=number, has_side_effects=True),
-    )(sums)
-
-
-def hour_kernel(n, in_ref, out_ref, arrived, send_sem, recv_sem):
-    me = lax.axis_index("hour")
-    order = [n // 2] + [d for d in range(1, n) if d != n // 2]
-
-    def copy(d):
-        return remote(in_ref, arrived.at[d], send_sem.at[d], recv_sem.at[d], hour=lax.rem(me + d, n))
-
-    peers = [lax.rem(me + d, n) for d in order]
-    pl.semaphore_wait(pltpu.get_barrier_semaphore(), greet("hour", peers))
-    for d in order:
-        copy(d).start()
-    arrived[0] = in_ref[...]
-    for d in order:
-        copy(d).wait()
-    out_ref[...] = jnp.sum(arrived[...], axis=0)
-
-
-def hour_total(x, number):
-    n = lax.axis_size("hour")
-    dma = pltpu.SemaphoreType.DMA
-    return pl.pallas_call(
-        lambda *refs: hour_kernel(n, *refs),
-        out_shape=jax.ShapeDtypeStruct(x.shape, jnp.float32),
-        in_specs=vmem(1),
-        out_specs=vmem(1)[0],
-        scratch_shapes=[pltpu.VMEM((n, *x.shape), jnp.float32), dma((n,)), dma((n,))],
-        compiler_params=pltpu.CompilerParams(collective_id=number, has_side_effects=True),
-    )(x)
-
-
-def samp_kernel(in_ref, out_ref, first, middle, second, send_y, recv_y, send_z, recv_z):
+def second_kernel(
+    n, sample_count, space_count, real,
+    in_ref, gap_ref, beta_ref, image_ref, place_ref, prof_ref, mine_ref, out_ref,
+    got, acc, square, part, arrived, owned, fresh, held, total, landed, first, middle, second, start,
+    *sems,
+):
     me = lax.axis_index("samp")
     z, y = me // NY, lax.rem(me, NY)
     far_first = sorted(range(1, NZ), key=lambda d: -min(d, NZ - d))
+    rows = image_ref.shape[0]
+    send_y, recv_y, send_z, recv_z = sems[10:]
 
     def y_copy(d):
-        return remote(in_ref, first.at[d], send_y.at[d], recv_y.at[d], samp=at_place(z, y + d))
+        return remote(start, first.at[d], send_y.at[d], recv_y.at[d], samp=at_place(z, y + d))
 
     def z_copy(d):
         return remote(middle, second.at[d], send_z.at[d], recv_z.at[d], samp=at_place(z + d, y))
 
     peers = [at_place(z + d, y) for d in far_first] + [at_place(z, y + d) for d in (2, 1, 3)]
-    pl.semaphore_wait(pltpu.get_barrier_semaphore(), greet("samp", peers))
+    count = greet("samp", peers) + greet_hours(n)
+    pl.semaphore_wait(pltpu.get_barrier_semaphore(), count)
+    scatter_body(in_ref, owned, held, total, landed, *sems[:4])
+    alpha_one = jnp.sqrt(owned[pl.ds(real, 1)] / sample_count + epsilon)
+    beta_one = beta_ref[pl.ds(0, 1)]
+    mismatch = owned[...] / alpha_one - (alpha_one / beta_one) * gap_ref[...]
+    row = lax.broadcasted_iota(jnp.int32, mismatch.shape, 0)
+    mismatch = jnp.where(row < real, mismatch, 0.0)
+    fresh[...] = mismatch
+    mine_ref[pl.ds(0, PAD)] = mismatch
+    mine_ref[pl.ds(PAD, 8)] = jnp.broadcast_to(alpha_one, (8, 128))
+    gather_body(spread_into(acc, square, got, place_ref), fresh, got, *sems[4:8])
+    fold(acc, square, prof_ref, part)
+    whole = hour_body(n, part, arrived, *sems[8:10])
+    beta_two = jnp.sqrt(whole[rows:rows + 1] / space_count + epsilon)
+    image_two = whole[:rows] / beta_two - beta_two * (image_ref[...] / alpha_one)
+    out_ref[pl.ds(0, rows)] = image_two
+    out_ref[pl.ds(rows, 8)] = whole[rows:]
+    start[...] = jnp.full(start.shape, jnp.sum(image_two * image_two))
     for d in (2, 1, 3):
         y_copy(d).start()
-    first[0] = in_ref[...]
+    first[0] = start[...]
     for d in (1, 3, 2):
         y_copy(d).wait()
     middle[...] = jnp.sum(first[...], axis=0)
@@ -269,24 +320,38 @@
     second[0] = middle[...]
     for d in far_first[::-1]:
         z_copy(d).wait()
-    out_ref[...] = jnp.sum(second[...], axis=0)
-
-
-def samp_total(x, number):
+    out_ref[pl.ds(rows + 8, 8)] = jnp.sum(second[...], axis=0)
+
+
+def second_totals(sums, gap, beta, image, place, profiles, sample_count, space_count, real, number):
+    n = lax.axis_size("hour")
+    uses, _, width = profiles.shape
+    block, small = sums.shape[1:], (8, 128)
     dma = pltpu.SemaphoreType.DMA
     return pl.pallas_call(
-        samp_kernel,
-        out_shape=jax.ShapeDtypeStruct(x.shape, jnp.float32),
-        in_specs=vmem(1),
-        out_specs=vmem(1)[0],
+        lambda *refs: second_kernel(n, sample_count, space_count, real, *refs),
+        out_shape=[
+            jax.ShapeDtypeStruct((PAD + 8, block[1]), jnp.float32),
+            jax.ShapeDtypeStruct((image.shape[0] + 16, 128), jnp.float32),
+        ],
+        in_specs=vmem(6),
+        out_specs=vmem(2),
         scratch_shapes=[
-            pltpu.VMEM((NY, *x.shape), jnp.float32),
-            pltpu.VMEM(x.shape, jnp.float32),
-            pltpu.VMEM((NZ, *x.shape), jnp.float32),
+            *spread_scratch(n, width, uses),
+            pltpu.VMEM(block, jnp.float32),
+            pltpu.VMEM(block, jnp.float32),
+            pltpu.VMEM((2, UP, NY, *block), jnp.float32),
+            pltpu.VMEM((NY, *block), jnp.float32),
+            pltpu.VMEM((NY, *block), jnp.float32),
+            pltpu.VMEM((NY, *small), jnp.float32),
+            pltpu.VMEM(small, jnp.float32),
+            pltpu.VMEM((NZ, *small), jnp.float32),
+            pltpu.VMEM(small, jnp.float32),
+            *gather_sems(), *gather_sems(), dma((n,)), dma((n,)),
             dma((NY,)), dma((NY,)), dma((NZ,)), dma((NZ,)),
         ],
         compiler_params=pltpu.CompilerParams(collective_id=number, has_side_effects=True),
-    )(x)
+    )(sums, gap, beta, image, place, profiles)
 
 
 def two_pieces(x, axis):
@@ -306,7 +371,10 @@
     space_count = float(per_owner * owners * row_width * hour_count)
     sample_count = float(use_count * samp_dev * owners)
     my_counties = lax.dynamic_index_in_dim(slot_county, owner_index, 0, keepdims=False)
-    county = jnp.take(my_counties, slot_of_sample)
+    slots = jnp.arange(slot_county.shape[1], dtype=jnp.int32)
+    county = jnp.sum(
+        jnp.where(slots[:, None] == slot_of_sample[None, :], my_counties[:, None], 0), axis=0
+    )
     place = county // per_owner * PAD + county % per_owner
     places = jnp.arange(owners * PAD, dtype=jnp.int32)
     onehot = (places[:, None] == place[None, :]).astype(jnp.bfloat16)
@@ -315,24 +383,12 @@
     def padded(rows):
         return jnp.pad(rows, ((0, PAD - per_owner), (0, 0)))
 
-    def backward(rows, number):
-        everyone = everyone_of(padded(rows), number)
-        square = jnp.sum(everyone * everyone)
-        pieces = two_pieces(everyone, 1)
-        spread = lax.dot_general(
-            pieces, onehot, (((0,), (0,)), ((), ())), preferred_element_type=jnp.float32
-        )
-        spread = (spread[:row_width] + spread[row_width:]).reshape(use_count, hour_dev, samp_dev)
-        partial = jnp.sum(wide * spread, axis=1)
-        rest = jnp.full((8, 128), square)
-        total = hour_total(jnp.concatenate([partial.reshape(-1, 128), rest], axis=0), number + 1)
-        return total[:-8].reshape(use_count, samp_dev), total[-1, 0]
-
     def my_share(x):
         return lax.dynamic_slice_in_dim(x, hour_index * share_len, share_len, 1)
 
     gap_rows = load_gap.reshape(per_owner, row_width)
-    plain, gap_total = backward(gap_rows, 1)
+    total = first_total(padded(gap_rows), place[None], profiles, 1)
+    plain, gap_total = total[:-8].reshape(use_count, samp_dev), total[-1, 0]
     beta_one = jnp.sqrt(gap_total / space_count + epsilon)
     image = plain / beta_one
     weighted = (wide * image[:, None, :]).reshape(row_width, samp_dev)
@@ -343,16 +399,16 @@
     mine = jnp.sum(image * image)
     row = jnp.arange(PAD, dtype=jnp.int32)[None, :, None]
     sums = jnp.where(row == per_owner, mine, sums)
-    owned = owned_of(sums, 5)
-    alpha_one = jnp.sqrt(owned[per_owner, 0] / sample_count + epsilon)
-    mismatch = owned[:per_owner] / alpha_one - (alpha_one / beta_one) * gap_rows
-    back, mismatch_total = backward(mismatch, 3)
-    beta_two = jnp.sqrt(mismatch_total / space_count + epsilon)
+    owned, last = second_totals(
+        sums, padded(gap_rows), jnp.full((8, 128), beta_one), total[:-8] / beta_one, place[None],
+        profiles, sample_count, space_count, per_owner, 2,
+    )
+    mismatch, alpha_one = owned[:per_owner], owned[PAD, 0]
+    vector_one = image / alpha_one
+    beta_two = jnp.sqrt(last[-16, 0] / space_count + epsilon)
+    alpha_two = jnp.sqrt(last[-1, 0] / sample_count + epsilon)
+    image_two = last[:-16].reshape(use_count, samp_dev)
     load_dir = mismatch / beta_two
-    vector_one = image / alpha_one
-    image_two = back / beta_two - beta_two * vector_one
-    second_total = samp_total(jnp.full((8, 128), jnp.sum(image_two * image_two)), 6)[0, 0]
-    alpha_two = jnp.sqrt(second_total / sample_count + epsilon)
     rho_value = jnp.sqrt(alpha_one * alpha_one + beta_two * beta_two)
     cosine = alpha_one / rho_value
     sine = beta_two / rho_value

time: 206 us -> 165 us (0.80)
  Pallas kernels: 153 us -> 137 us
  local copies, waits for them, and re-layouts: 20.2 us -> 8.25 us
  matrix products: 14.8 us -> 4.89 us
  other arithmetic: 13.4 us -> 8.61 us
    pallas_call x6 -> x2, Pallas kernels: 153 us -> 137 us  [the longest x1 83.5 us: second_totals(): pl.pallas_call(lambda *refs: second_kernel(n, sample_count, space_count,...]
    dot_general x2 -> x0, matrix products: 9.88 us -> none  [backward(): lax.dot_general(pieces, onehot, (((0,), (0,)), ((), ())), preferred_eleme...]
    gather x1 -> x0, local copies, waits for them, and re-layouts: 8.58 us -> none  [local(): county = jnp.take(my_counties, slot_of_sample)]
    reduce_sum x5 -> x1, other arithmetic: 7.06 us -> 1.78 us  [local(): jnp.sum(jnp.where(slots[:, None] == slot_of_sample[None, :], my_counties[...]
    concatenate x2 -> x0, local copies, waits for them, and re-layouts: 2.52 us -> none  [backward(): jnp.concatenate([partial.reshape(-1, 128), rest], axis=0)]
where the time goes in v6:
time: 165 us; the launch traced here: 164 us
  Pallas kernels  137 us (83%)
  other arithmetic  8.61 us (5%)
  local copies, waits for them, and re-layouts  8.25 us (5%)
  between operations  5.57 us (3%)
  matrix products  4.89 us (3%)
    pallas_call x1, Pallas kernels, second_totals(): pl.pallas_call(lambda *refs: second_kernel(n, sample_count, space_count,...  83.5 us
    pallas_call x1, Pallas kernels, first_total(): pl.pallas_call(lambda *refs: first_kernel(n, *refs), out_shape=jax.ShapeD...  53 us
    dot_general x1, matrix products, local(): lax.dot_general(onehot, two_pieces(weighted, 0), (((1,), (1,)), ((), ()))...  4.89 us

profile of v6, /device:TPU:1, one launch (start us, length us, event | category | flops | bytes accessed | tf_op | source)
XLA Modules:
  0.0 163.9 jit_solution(5479499591220648386)
XLA Ops:
  0.6 0.0 copy-start
  0.7 0.9 copy-done
  1.6 1.8 %select_reduce_fusion = s32[2048]{0:T(1024)S(1)} fusion(s32[1024]{0:T(1024)S(1)} %bitcast.18, s32[2048]{0:T(1024)} %param.6), kind=kLoop, calls=%fused_computation.3 | loop fusion | flops 6289408 | bytes 20480 | tf_op jit(solution)/shard_map/reduce_sum | solution.py:375
  3.4 0.6 fusion.6.refs_1_.refs_4_
  4.0 0.9 copy.13
  5.0 0.6 pad.5.refs_0_.refs_1_
  5.6 53.0 %shard_map.67 = f32[72,128]{1,0:T(8,128)} custom-call(f32[48,128]{1,0:T(8,128)} %pad.5.refs_0_.refs_1_, s32[1,2048]{1,0:T(1,128)} %fusion.6.refs_1_.refs_4_, bf16[4,32,2048]{2,1,0:T(8,128)(2,1)} %refs_5_.1), custom_call_target="tpu_custom_call" | custom-call | tf_op jit(solution)/shard_map/pallas_call | solution.py:198
  58.6 1.2 slice.29
  60.5 1.4 multiply_reduce_fusion
  61.9 1.1 convert_multiply_fusion
  63.1 0.1 reduce-precision_convert_fusion
  63.2 4.9 %fusion = f32[3072,256]{1,0:T(8,128)S(1)} fusion(s32[2048]{0:T(1024)S(1)} %get-tuple-element.18, bf16[128,2048]{1,0:T(8,128)(2,1)S(1)} %get-tuple-element.21, bf16[128,2048]{1,0:T(8,128)(2,1)S(1)} %get-tuple-element.20), kind=kOutput, calls=%fused_computation.1 | convolution fusion | flops 3229614080 | bytes 4202496 | tf_op jit(solution)/shard_map/dot_general | solution.py:395
  68.1 0.0 copy-done.1
  68.1 0.2 slice_add_fusion
  68.3 0.0 copy-start.2
  68.3 2.0 %broadcast_select_fusion.refs_0_ = f32[64,48,128]{2,1,0:T(8,128)} fusion(f32[64,48,128]{2,1,0:T(8,128)S(1)} %bitcast.13, f32[]{:T(128)} %get-tuple-element.16, pred[48]{0:T(512)(128)(4,1)S(1)} %iota_compare_fusion.3), kind=kLoop, calls=%fused_computation.13 | loop fusion | flops 393216 | bytes 3145780 | tf_op jit(solution)/shard_map/jit(_where)/select_n | solution.py:401
  70.3 0.6 broadcast_in_dim.43.refs_2_
  70.9 83.5 %shard_map.68 = (f32[56,128]{1,0:T(8,128)}, f32[80,128]{1,0:T(8,128)}) custom-call(f32[64,48,128]{2,1,0:T(8,128)} %broadcast_select_fusion.refs_0_, f32[48,128]{1,0:T(8,128)} %pad.5.refs_0_.refs_1_, f32[8,128]{1,0:T(8,128)} %broadcast_in_dim.43.refs_2_, f32[64,128]{1,0:T(8,128)} %copy-done.1, s32[1,2048]{1,0:T(1,128)} %fusion.6.refs_1_.refs_4_, ...), custom_call_target="tpu_custom_call" | custom-call | tf_op jit(solution)/shard_map/pallas_call | solution.py:331
  154.4 1.2 fusion.10
  156.3 0.7 slice_divide_fusion.2
  157.1 0.7 copy.14
  157.8 1.2 slice.32
  162.5 0.8 slice.34
  163.3 0.6 divide_subtract_fusion
  (9 shorter events, 0.1 us)
Async XLA Ops:
  0.6 1.0 copy-start
  61.9 6.2 %copy-start.1 = (f32[64,128]{1,0:T(8,128)}, f32[64,128]{1,0:T(8,128)S(1)}, u32[]{:S(2)}) copy-start(f32[64,128]{1,0:T(8,128)S(1)} %get-tuple-element.17.refs_3_) | copy-start | bytes 98308
  68.3 94.2 %copy-start.2 = (f32[72,128]{1,0:T(8,128)S(1)}, f32[72,128]{1,0:T(8,128)}, u32[]{:S(2)}) copy-start(f32[72,128]{1,0:T(8,128)} %shard_map.67) | copy-start | bytes 110596

commit v7 on v6

--- a/solution.py
+++ b/solution.py
@@ -273,8 +273,8 @@
 
 def second_kernel(
     n, sample_count, space_count, real,
-    in_ref, gap_ref, beta_ref, image_ref, place_ref, prof_ref, mine_ref, out_ref,
-    got, acc, square, part, arrived, owned, fresh, held, total, landed, first, middle, second, start,
+    in_ref, gap_ref, beta_ref, image_ref, place_ref, prof_ref, load_ref, step_ref, dir_ref,
+    kept, got, acc, square, part, arrived, owned, fresh, held, total, landed, first, middle, second, start,
     *sems,
 ):
     me = lax.axis_index("samp")
@@ -299,15 +299,13 @@
     row = lax.broadcasted_iota(jnp.int32, mismatch.shape, 0)
     mismatch = jnp.where(row < real, mismatch, 0.0)
     fresh[...] = mismatch
-    mine_ref[pl.ds(0, PAD)] = mismatch
-    mine_ref[pl.ds(PAD, 8)] = jnp.broadcast_to(alpha_one, (8, 128))
     gather_body(spread_into(acc, square, got, place_ref), fresh, got, *sems[4:8])
     fold(acc, square, prof_ref, part)
     whole = hour_body(n, part, arrived, *sems[8:10])
     beta_two = jnp.sqrt(whole[rows:rows + 1] / space_count + epsilon)
     image_two = whole[:rows] / beta_two - beta_two * (image_ref[...] / alpha_one)
-    out_ref[pl.ds(0, rows)] = image_two
-    out_ref[pl.ds(rows, 8)] = whole[rows:]
+    kept[...] = image_two
+    load_ref[...] = mismatch / beta_two
     start[...] = jnp.full(start.shape, jnp.sum(image_two * image_two))
     for d in (2, 1, 3):
         y_copy(d).start()
@@ -320,7 +318,20 @@
     second[0] = middle[...]
     for d in far_first[::-1]:
         z_copy(d).wait()
-    out_ref[pl.ds(rows + 8, 8)] = jnp.sum(second[...], axis=0)
+    alpha_two = jnp.sqrt(jnp.sum(second[...], axis=0)[:1] / sample_count + epsilon)
+    rho_value = jnp.sqrt(alpha_one * alpha_one + beta_two * beta_two)
+    cosine = alpha_one / rho_value
+    sine = beta_two / rho_value
+    uses = prof_ref.shape[0]
+    each = rows // uses
+    share = each // n
+    for e in range(uses):
+        spot = pl.ds(e * each + lax.axis_index("hour") * share, share)
+        vector_one = image_ref[spot] / alpha_one
+        step_ref[pl.ds(e * share, share)] = cosine * beta_one / rho_value * vector_one
+        dir_ref[pl.ds(e * share, share)] = (
+            kept[spot] / alpha_two - sine * alpha_two / rho_value * vector_one
+        )
 
 
 def second_totals(sums, gap, beta, image, place, profiles, sample_count, space_count, real, number):
@@ -331,12 +342,14 @@
     return pl.pallas_call(
         lambda *refs: second_kernel(n, sample_count, space_count, real, *refs),
         out_shape=[
-            jax.ShapeDtypeStruct((PAD + 8, block[1]), jnp.float32),
-            jax.ShapeDtypeStruct((image.shape[0] + 16, 128), jnp.float32),
+            jax.ShapeDtypeStruct(block, jnp.float32),
+            jax.ShapeDtypeStruct((image.shape[0] // n, 128), jnp.float32),
+            jax.ShapeDtypeStruct((image.shape[0] // n, 128), jnp.float32),
         ],
         in_specs=vmem(6),
-        out_specs=vmem(2),
+        out_specs=vmem(3),
         scratch_shapes=[
+            pltpu.VMEM(image.shape, jnp.float32),
             *spread_scratch(n, width, uses),
             pltpu.VMEM(block, jnp.float32),
             pltpu.VMEM(block, jnp.float32),
@@ -363,7 +376,6 @@
     owners = lax.axis_size("samp")
     hour_count = lax.axis_size("hour")
     owner_index = lax.axis_index("samp")
-    hour_index = lax.axis_index("hour")
     use_count, hour_dev, samp_dev = profiles.shape
     per_owner = load_gap.shape[0]
     row_width = use_count * hour_dev
@@ -383,9 +395,6 @@
     def padded(rows):
         return jnp.pad(rows, ((0, PAD - per_owner), (0, 0)))
 
-    def my_share(x):
-        return lax.dynamic_slice_in_dim(x, hour_index * share_len, share_len, 1)
-
     gap_rows = load_gap.reshape(per_owner, row_width)
     total = first_total(padded(gap_rows), place[None], profiles, 1)
     plain, gap_total = total[:-8].reshape(use_count, samp_dev), total[-1, 0]
@@ -399,23 +408,15 @@
     mine = jnp.sum(image * image)
     row = jnp.arange(PAD, dtype=jnp.int32)[None, :, None]
     sums = jnp.where(row == per_owner, mine, sums)
-    owned, last = second_totals(
+    load_dir, weight_step, search_dir = second_totals(
         sums, padded(gap_rows), jnp.full((8, 128), beta_one), total[:-8] / beta_one, place[None],
         profiles, sample_count, space_count, per_owner, 2,
     )
-    mismatch, alpha_one = owned[:per_owner], owned[PAD, 0]
-    vector_one = image / alpha_one
-    beta_two = jnp.sqrt(last[-16, 0] / space_count + epsilon)
-    alpha_two = jnp.sqrt(last[-1, 0] / sample_count + epsilon)
-    image_two = last[:-16].reshape(use_count, samp_dev)
-    load_dir = mismatch / beta_two
-    rho_value = jnp.sqrt(alpha_one * alpha_one + beta_two * beta_two)
-    cosine = alpha_one / rho_value
-    sine = beta_two / rho_value
-    vector_share = my_share(vector_one)
-    weight_step = cosine * beta_one / rho_value * vector_share
-    search_dir = my_share(image_two) / alpha_two - sine * alpha_two / rho_value * vector_share
-    return (weight_step, search_dir, load_dir.reshape(per_owner, use_count, hour_dev))
+    return (
+        weight_step.reshape(use_count, share_len),
+        search_dir.reshape(use_count, share_len),
+        load_dir[:per_owner].reshape(per_owner, use_count, hour_dev),
+    )
 
 
 def solution(mesh):

time: 165 us -> 160 us (0.970)
  between operations: 5.57 us -> 1.42 us
    slice x3 -> x0, local copies, waits for them, and re-layouts: 3.19 us -> none  [the longest x1 1.24 us: local(): alpha_two = jnp.sqrt(last[-1, 0] / sample_count + epsilon)]
    reshape x1 -> x2, local copies, waits for them, and re-layouts: 0.02 us -> 2.56 us  [the longest x1 1.28 us: local(): weight_step.reshape(use_count, share_len)]
where the time goes in v7:
time: 160 us; the launch traced here: 159 us
  Pallas kernels  137 us (86%)
  local copies, waits for them, and re-layouts  8.33 us (5%)
  other arithmetic  7.23 us (5%)
  matrix products  4.89 us (3%)
    pallas_call x1, Pallas kernels, second_totals(): pl.pallas_call(lambda *refs: second_kernel(n, sample_count, space_count,...  83.8 us
    pallas_call x1, Pallas kernels, first_total(): pl.pallas_call(lambda *refs: first_kernel(n, *refs), out_shape=jax.ShapeD...  53.1 us
    dot_general x1, matrix products, local(): lax.dot_general(onehot, two_pieces(weighted, 0), (((1,), (1,)), ((), ()))...  4.89 us

profile of v7, /device:TPU:1, one launch (start us, length us, event | category | flops | bytes accessed | tf_op | source)
XLA Modules:
  0.0 158.8 jit_solution(9696546081710255562)
XLA Ops:
  0.6 0.0 copy-start
  0.6 0.9 copy-done
  1.6 1.8 %select_reduce_fusion = s32[2048]{0:T(1024)S(1)} fusion(s32[1024]{0:T(1024)S(1)} %bitcast.17, s32[2048]{0:T(1024)} %param.6), kind=kLoop, calls=%fused_computation.3 | loop fusion | flops 6289408 | bytes 20480 | tf_op jit(solution)/shard_map/reduce_sum | solution.py:387
  3.4 0.6 fusion.6.refs_1_.refs_4_
  4.0 0.9 copy.13
  4.9 0.6 pad.5.refs_0_.refs_1_
  5.6 53.1 %shard_map.67 = f32[72,128]{1,0:T(8,128)} custom-call(f32[48,128]{1,0:T(8,128)} %pad.5.refs_0_.refs_1_, s32[1,2048]{1,0:T(1,128)} %fusion.6.refs_1_.refs_4_, bf16[4,32,2048]{2,1,0:T(8,128)(2,1)} %refs_5_.1), custom_call_target="tpu_custom_call" | custom-call | tf_op jit(solution)/shard_map/pallas_call | solution.py:198
  58.6 1.2 slice.17
  60.5 1.4 multiply_reduce_fusion
  61.9 0.0 copy-start.1
  61.9 1.1 convert_multiply_fusion
  63.1 0.1 reduce-precision_convert_fusion
  63.2 4.9 %fusion = f32[3072,256]{1,0:T(8,128)S(1)} fusion(s32[2048]{0:T(1024)S(1)} %get-tuple-element.26, bf16[128,2048]{1,0:T(8,128)(2,1)S(1)} %get-tuple-element.23, bf16[128,2048]{1,0:T(8,128)(2,1)S(1)} %get-tuple-element.22), kind=kOutput, calls=%fused_computation.1 | convolution fusion | flops 3229614080 | bytes 4202496 | tf_op jit(solution)/shard_map/dot_general | solution.py:404
  68.1 0.0 copy-done.1
  68.1 0.2 slice_add_fusion
  68.3 2.0 %broadcast_select_fusion.refs_0_ = f32[64,48,128]{2,1,0:T(8,128)} fusion(f32[64,48,128]{2,1,0:T(8,128)S(1)} %bitcast.11, f32[]{:T(128)} %get-tuple-element.18, pred[48]{0:T(512)(128)(4,1)S(1)} %iota_compare_fusion.3), kind=kLoop, calls=%fused_computation.13 | loop fusion | flops 393216 | bytes 3145780 | tf_op jit(solution)/shard_map/jit(_where)/select_n | solution.py:410
  70.3 0.6 broadcast_in_dim.43.refs_2_
  70.9 83.8 %shard_map.68 = (f32[48,128]{1,0:T(8,128)}, f32[8,128]{1,0:T(8,128)}, f32[8,128]{1,0:T(8,128)}) custom-call(f32[64,48,128]{2,1,0:T(8,128)} %broadcast_select_fusion.refs_0_, f32[48,128]{1,0:T(8,128)} %pad.5.refs_0_.refs_1_, f32[8,128]{1,0:T(8,128)} %broadcast_in_dim.43.refs_2_, f32[64,128]{1,0:T(8,128)} %copy-done.1, s32[1,2048]{1,0:T(1,128)} %fusion.6.refs_1_.refs_4_, ...), custom_call_target="tpu_custom_call" | custom-call | tf_op jit(solution)/shard_map/pallas_call | solution.py:342
  154.7 1.5 copy.14
  156.2 1.3 reshape.101
  157.5 1.3 reshape.102
  (4 shorter events, 0.0 us)
Async XLA Ops:
  0.6 1.0 copy-start
  61.9 6.2 %copy-start.1 = (f32[64,128]{1,0:T(8,128)}, f32[64,128]{1,0:T(8,128)S(1)}, u32[]{:S(2)}) copy-start(f32[64,128]{1,0:T(8,128)S(1)} %get-tuple-element.19.refs_3_) | copy-start | bytes 98308
